TPU v7x, 128 devices: a whole 4x4x4 slice. The times are simulated.
128 devices in a mesh: src: 32 (over y, z, core), rcv: 4 (over x).
Axes of the slice: x: 4, y: 4, z: 4, core: 2. Of those that a mesh axis runs over, the one named last changes fastest.
Arguments:
- traces: bfloat16 [262144, 2048], P(('src', 'rcv'))
- trace_source: int32 [262144], P(('src', 'rcv')), may hold values from 0 to 255, as said below
- trace_offset: int32 [262144], P(('src', 'rcv')), may hold values from 0 to 63
- trace_slot: int32 [262144], P(('src', 'rcv')), may hold values from 0 to 1023, as said below
- request_list: int32 [128, 128, 8], P(('src', 'rcv')), may hold values from 0 to 63, as said below
- source_terms: float32 [256, 1024], P('src'), may hold values from -3 to 3
- receiver_terms: float32 [8192, 1024], P(('src', 'rcv')), may hold values from -3 to 3
- offset_terms: float32 [64, 1024], replicated, may hold values from -3 to 3
Outputs:
- source_new: float32 [256, 1024], P('src')
- receiver_new: float32 [8192, 1024], P(('src', 'rcv'))
- offset_new: float32 [64, 1024], replicated
Inputs may be any that keep to these rules, and one draw needn't show every extreme that they name: `trace_source`: trace t's source is one of the 8 sources of the src index that holds t. `request_list`: within one device's list for one owner the 8 entries are distinct. `trace_slot`: a slot names an owner and a position in the holding device's own request list.
All inputs are finite; a program needn't handle non-finite values.
Results may differ from a plain program's by a relative error of at most 0.0023.
Values sent between devices are 32-bit elements; how exact they have to be, the bound alone decides.
A program may use at most 128 MiB of HBM per device.

v0:
```python
import math

import jax
import jax.numpy as jnp
from jax import lax
from jax.sharding import PartitionSpec as P


def dft_table(samples):
    freq = samples // 2
    index_n = lax.broadcasted_iota(jnp.int32, (samples, freq), 0)
    index_f = lax.broadcasted_iota(jnp.int32, (samples, freq), 1)
    phase = (index_n * index_f % samples).astype(jnp.float32) * (2.0 * math.pi / samples)
    taper = 0.5 - 0.5 * jnp.cos((index_n.astype(jnp.float32) + 0.5) * (2.0 * math.pi / samples))
    scaled = taper / math.sqrt(samples)
    return jnp.concatenate([scaled * jnp.cos(phase), -scaled * jnp.sin(phase)], axis=1).astype(
        jnp.bfloat16
    )


def collect(one_hot, residual):
    upper = residual.astype(jnp.bfloat16)
    lower = (residual - upper.astype(jnp.float32)).astype(jnp.bfloat16)
    dims = (((0,), (0,)), ((), ()))
    first = lax.dot_general(one_hot, upper, dims, preferred_element_type=jnp.float32)
    second = lax.dot_general(one_hot, lower, dims, preferred_element_type=jnp.float32)
    return first + second


def local(
    traces,
    trace_source,
    trace_offset,
    trace_slot,
    request_list,
    source_terms,
    receiver_terms,
    offset_terms,
):
    peers = lax.axis_size(("src", "rcv"))
    slots = request_list.shape[2]
    freq = receiver_terms.shape[1]
    owned = receiver_terms.shape[0]
    requests = request_list.reshape(peers, slots)
    asked = lax.all_to_all(requests, ("src", "rcv"), split_axis=0, concat_axis=0, tiled=True)
    served = receiver_terms[asked.reshape(-1)].reshape(peers, slots, freq)
    fetched = lax.all_to_all(
        served, ("src", "rcv"), split_axis=0, concat_axis=0, tiled=True
    ).reshape(peers * slots, freq)
    table = dft_table(traces.shape[1])
    spectra = jnp.dot(traces, table, preferred_element_type=jnp.float32)
    real_part = spectra[:, :freq]
    imag_part = spectra[:, freq:]
    logamp = 0.5 * jnp.log(real_part * real_part + imag_part * imag_part + 0.01)
    num_src = source_terms.shape[0]
    num_off = offset_terms.shape[0]
    src_local = trace_source - lax.axis_index("src") * num_src
    residual = logamp - source_terms[src_local] - fetched[trace_slot] - offset_terms[trace_offset]
    ones = jnp.ones((traces.shape[0],), jnp.float32)
    rcv_part = jax.ops.segment_sum(residual, trace_slot, num_segments=peers * slots).reshape(
        peers, slots, freq
    )
    rcv_cnt = jax.ops.segment_sum(ones, trace_slot, num_segments=peers * slots).reshape(
        peers, slots
    )
    got_part, got_cnt = (
        lax.all_to_all(rcv_part, ("src", "rcv"), split_axis=0, concat_axis=0, tiled=True),
        lax.all_to_all(rcv_cnt, ("src", "rcv"), split_axis=0, concat_axis=0, tiled=True),
    )
    flat_asked = asked.reshape(-1)
    rcv_grad = jax.ops.segment_sum(
        got_part.reshape(peers * slots, freq), flat_asked, num_segments=owned
    )
    rcv_total = jax.ops.segment_sum(got_cnt.reshape(peers * slots), flat_asked, num_segments=owned)
    receiver_new = receiver_terms + rcv_grad / (rcv_total + 1.0)[:, None]
    columns = jnp.arange(num_src + num_off, dtype=jnp.int32)[None, :]
    both_hot = (
        (src_local[:, None] == columns) | ((trace_offset + num_src)[:, None] == columns)
    ).astype(jnp.bfloat16)
    joint = collect(both_hot, residual)
    joint_cnt = jnp.sum(both_hot.astype(jnp.float32), axis=0)
    src_part = joint[:num_src]
    off_part = joint[num_src:]
    src_cnt = joint_cnt[:num_src]
    off_cnt = joint_cnt[num_src:]
    src_sum, src_tot = lax.psum((src_part, src_cnt), "rcv")
    off_sum, off_tot = lax.psum((off_part, off_cnt), ("src", "rcv"))
    source_new = source_terms + src_sum / (src_tot + 1.0)[:, None]
    offset_new = offset_terms + off_sum / (off_tot + 1.0)[:, None]
    return (source_new, receiver_new, offset_new)


def solution(mesh):
    return jax.shard_map(
        local,
        mesh=mesh,
        in_specs=(
            P(("src", "rcv"), None),
            P(("src", "rcv")),
            P(("src", "rcv")),
            P(("src", "rcv")),
            P(("src", "rcv"), None, None),
            P("src", None),
            P(("src", "rcv"), None),
            P(),
        ),
        out_specs=(P("src", None), P(("src", "rcv"), None), P()),
        check_vma=False,
    )
```

profile of v0, /device:TPU:1, one launch (start us, length us, event | category | flops | bytes accessed | tf_op | source)
XLA Modules:
  0.0 526.6 jit_solution(12145871328240511562)
XLA Ops:
  7.2 1.4 copy.27
  8.6 11.5 %all-to-all-start = ((s32[128,1,8]{2,1,0:T(1,128)}), s32[128,1,8]{2,1,0:T(1,128)S(1)}, u32[]{:S(2)}, u32[]{:S(2)}) async-start(s32[128,1,8]{2,1,0:T(1,128)} %bitcast.1), calls=%async_computation | async-start | bytes 131072 | tf_op jit(solution)/shard_map/all_to_all | solution.py:45
  20.1 0.1 fusion.39
  20.2 0.7 fusion.37
  20.9 0.7 fusion.36
  21.6 0.1 subtract_multiply_fusion
  21.7 14.8 %scatter_custom_fusion.2 = f32[1024]{0:T(1024)S(1)} fusion(s32[2048]{0:T(1024)} %param.11, f32[2048]{0:T(1024)S(1)} %broadcast.70, f32[]{:T(128)} %constant.12.clone.1), kind=kCustom, calls=%fused_computation.67 | custom fusion | flops 2048 | bytes 4608 | tf_op jit(solution)/shard_map/scatter-add | solution.py:63
  36.5 0.7 all_to_all.22
  37.2 9.8 %gather_fusion = f32[2048,1024]{1,0:T(8,128)} fusion(f32[8,1024]{1,0:T(8,128)S(1)} %copy-done, s32[2048]{0:T(1024)S(1)} %get-tuple-element.5), kind=kCustom, calls=%fused_computation | custom fusion | bytes 16785408 | tf_op jit(solution)/shard_map/gather | solution.py:58
  47.0 9.2 %copy.26 = f32[2048,1024]{0,1:T(8,128)} copy(f32[2048,1024]{1,0:T(8,128)} %gather_fusion) | data formatting | bytes 16777216 | tf_op jit(solution)/shard_map/gather | solution.py:58
  56.2 9.8 %gather_fusion.3 = f32[2048,1024]{1,0:T(8,128)} fusion(f32[64,1024]{1,0:T(8,128)S(1)} %copy-done.1, s32[2048]{0:T(1024)S(1)} %get-tuple-element.11), kind=kCustom, calls=%fused_computation.3 | custom fusion | bytes 16785408 | tf_op jit(solution)/shard_map/gather | solution.py:58
  66.0 9.2 %copy.29 = f32[2048,1024]{0,1:T(8,128)} copy(f32[2048,1024]{1,0:T(8,128)} %gather_fusion.3) | data formatting | bytes 16777216 | tf_op jit(solution)/shard_map/gather | solution.py:58
  75.2 0.0 all-to-all-done
  75.2 0.5 broadcast.118
  75.7 0.8 reduce.8
  76.5 0.1 reshape.68
  76.6 5.4 %gather_fusion.1 = f32[1024,1024]{1,0:T(8,128)} fusion(f32[64,1024]{1,0:T(8,128)S(1)} %copy-done.2, s32[1024]{0:T(1024)S(1)} %broadcast_clamp_fusion), kind=kCustom, calls=%fused_computation.1 | custom fusion | bytes 8392704 | tf_op jit(solution)/shard_map/gather | solution.py:46
  82.1 10.2 %all-to-all-start.1 = ((f32[128,8,1024]{2,1,0:T(8,128)}), f32[128,8,1024]{2,1,0:T(8,128)}, u32[]{:S(2)}, u32[]{:S(2)}) async-start(f32[128,8,1024]{2,1,0:T(8,128)} %bitcast.14), calls=%async_computation.1 | async-start | bytes 8388608 | tf_op jit(solution)/shard_map/all_to_all | solution.py:47
  92.3 34.8 %multiply_convert_fusion = (bf16[2048,1024]{1,0:T(8,128)(2,1)S(1)}, bf16[2048,1024]{1,0:T(8,128)(2,1)S(1)}) fusion(f32[2048]{0:T(1024)S(1)} %fusion.39, f32[2048]{0:T(1024)S(1)} %subtract_multiply_fusion), kind=kLoop, calls=%fused_computation.28 | loop fusion | flops 37748736 | bytes 8404992 | tf_op jit(solution)/shard_map/convert.1
  127.0 21.9 %convolution_bitcast_fusion = f32[2048,2048]{0,1:T(8,128)} fusion(bf16[2048,2048]{1,0:T(8,128)(2,1)} %param.8, bf16[2048,1024]{1,0:T(8,128)(2,1)S(1)} %get-tuple-element.9, bf16[2048,1024]{1,0:T(8,128)(2,1)S(1)} %get-tuple-element.10), kind=kOutput, calls=%fused_computation.11 | convolution fusion | flops 17196646400 | bytes 33554432 | tf_op jit(solution)/shard_map/dot_general | solution.py:51
  149.0 0.0 all-to-all-done.1
  149.0 9.8 %all-to-all-start.3 = ((f32[128,1,8]{2,1,0:T(1,128)}), f32[128,1,8]{2,1,0:T(1,128)S(1)}, u32[]{:S(2)}, u32[]{:S(2)}) async-start(f32[128,1,8]{2,1,0:T(1,128)} %bitcast.7), calls=%async_computation.3 | async-start | bytes 131072 | tf_op jit(solution)/shard_map/all_to_all | solution.py:68
  158.8 13.9 %gather_fusion.2 = f32[2048,1024]{1,0:T(8,128)} fusion(f32[1024,1024]{1,0:T(8,128)} %bitcast.4, s32[2048]{0:T(1024)S(1)} %fusion.37), kind=kCustom, calls=%fused_computation.2 | custom fusion | bytes 16785408 | tf_op jit(solution)/shard_map/gather | solution.py:58
  172.6 9.1 %copy.28 = f32[2048,1024]{0,1:T(8,128)} copy(f32[2048,1024]{1,0:T(8,128)} %gather_fusion.2) | data formatting | bytes 16777216 | tf_op jit(solution)/shard_map/gather | solution.py:58
  181.7 19.4 %fusion.9 = f32[2048,1024]{0,1:T(8,128)} fusion(f32[2048,1024]{0,1:T(8,128)} %copy.29, f32[2048,1024]{0,1:T(8,128)} %copy.28, f32[2048,1024]{0,1:T(8,128)} %copy.26, f32[2048,2048]{0,1:T(8,128)} %convolution_bitcast_fusion), kind=kLoop, calls=%fused_computation.22 | loop fusion | flops 16777216 | bytes 50331648 | tf_op jit(solution)/shard_map/sub | solution.py:58
  201.1 9.3 %copy.30 = f32[2048,1024]{1,0:T(8,128)} copy(f32[2048,1024]{0,1:T(8,128)} %fusion.9) | data formatting | bytes 16777216 | tf_op jit(solution)/shard_map/sub | solution.py:58
  210.4 21.2 %scatter_custom_fusion = f32[1024,1024]{1,0:T(8,128)} fusion(s32[2048]{0:T(1024)} %param.11, f32[2048,1024]{1,0:T(8,128)} %copy.30, f32[]{:T(128)} %constant.12.clone.1), kind=kCustom, calls=%fused_computation.36 | custom fusion | flops 2097152 | bytes 4194816 | tf_op jit(solution)/shard_map/scatter-add | solution.py:60
  231.5 0.0 all-to-all-done.3
  231.5 10.2 %all-to-all-start.2 = ((f32[128,8,1024]{2,1,0:T(8,128)}), f32[128,8,1024]{2,1,0:T(8,128)}, u32[]{:S(2)}, u32[]{:S(2)}) async-start(f32[128,8,1024]{2,1,0:T(8,128)} %bitcast.15), calls=%async_computation.2 | async-start | bytes 8388608 | tf_op jit(solution)/shard_map/all_to_all | solution.py:67
  241.7 0.0 all-reduce.3.cloned.1.call-start
  241.8 0.2 convert_reduce_fusion
  242.0 0.1 slice.23
  242.1 103.8 %psum.31 = f32[64]{0:T(128)S(1)} all-reduce(f32[64]{0:T(128)S(1)} %slice.23), channel_id=1, replica_groups=mesh['src'=32,'rcv'=4] {'src','rcv'}, use_global_device_ids=true, to_apply=%region_8.9 | all-reduce | flops 64 | bytes 512 | tf_op jit(solution)/shard_map/psum | solution.py:87
  345.9 0.5 broadcast.119
  346.4 0.8 reduce.9
  347.2 0.1 reshape.134
  347.3 0.1 reshape.116
  347.4 7.8 %scatter_custom_fusion.3 = f32[64]{0:T(128)S(1)} fusion(s32[1024]{0:T(1024)S(1)} %reshape.116, f32[1024]{0:T(1024)S(1)} %reshape.134, f32[]{:T(128)} %constant.13.clone.1), kind=kCustom, calls=%fused_computation.70 | custom fusion | flops 1024 | bytes 260 | tf_op jit(solution)/shard_map/scatter-add | solution.py:74
  355.2 7.2 %fusion.16 = f32[72,1024]{1,0:T(8,128)S(1)} fusion(f32[2048,1024]{0,1:T(8,128)} %fusion.9, s32[2048]{0:T(1024)S(1)} %get-tuple-element.12, s32[2048]{0:T(1024)S(1)} %get-tuple-element.6), kind=kOutput, calls=%fused_computation.33 | convolution fusion | flops 310820864 | bytes 8699904 | tf_op jit(solution)/shard_map/dot_general | solution.py:26
  362.4 4.8 fusion.24
  367.2 0.7 slice.35
  367.9 0.0 all-reduce.3.cloned.1.call-update
  368.0 13.2 %all-reduce = (f32[8,1024]{1,0:T(8,128)S(1)}, f32[8]{0:T(128)S(1)}) all-reduce(f32[8,1024]{1,0:T(8,128)S(1)} %slice.34, f32[8]{0:T(128)S(1)} %bitcast.18), channel_id=1, replica_groups=mesh['src'=32,'rcv'=4] {'rcv'}, use_global_device_ids=true, to_apply=%region_0.1 | all-reduce | flops 8200 | bytes 65600 | tf_op jit(solution)/shard_map/psum | solution.py:86
  381.1 0.7 divide_add_fusion.2
  381.8 125.3 %all-reduce.3.cloned.1.call-done = f32[64,1024]{1,0:T(8,128)} async-done(((f32[64,1024]{1,0:T(8,128)}), f32[64,1024]{1,0:T(8,128)}) %all-reduce.3.cloned.1.call-update) | async-done | bytes 262160 | tf_op jit(solution)/shard_map/psum | solution.py:87
  507.1 1.8 divide_add_fusion
  508.8 10.1 %scatter_custom_fusion.1 = f32[64,1024]{1,0:T(8,128)S(1)} fusion(s32[1024]{0:T(1024)S(1)} %reshape.116, f32[128,8,1024]{2,1,0:T(8,128)} %all-to-all-done.2, f32[]{:T(128)} %constant.12.clone.1), kind=kCustom, calls=%fused_computation.34 | custom fusion | flops 1048576 | bytes 4456452 | tf_op jit(solution)/shard_map/scatter-add | solution.py:71
  519.0 0.8 divide_add_fusion.1
  (13 shorter events, 0.0 us)
Async XLA Ops:
  7.2 30.0 %copy-start = (f32[8,1024]{1,0:T(8,128)S(1)}, f32[8,1024]{1,0:T(8,128)}, u32[]{:S(2)}) copy-start(f32[8,1024]{1,0:T(8,128)} %param.13) | copy-start | bytes 98308
  8.6 66.6 %all-to-all-start = ((s32[128,1,8]{2,1,0:T(1,128)}), s32[128,1,8]{2,1,0:T(1,128)S(1)}, u32[]{:S(2)}, u32[]{:S(2)}) async-start(s32[128,1,8]{2,1,0:T(1,128)} %bitcast.1), calls=%async_computation | async-start | bytes 131072 | tf_op jit(solution)/shard_map/all_to_all | solution.py:45
  47.0 9.2 %copy-start.1 = (f32[64,1024]{1,0:T(8,128)S(1)}, f32[64,1024]{1,0:T(8,128)}, u32[]{:S(2)}) copy-start(f32[64,1024]{1,0:T(8,128)} %param.15) | copy-start | bytes 786436
  66.0 10.6 %copy-start.2 = (f32[64,1024]{1,0:T(8,128)S(1)}, f32[64,1024]{1,0:T(8,128)}, u32[]{:S(2)}) copy-start(f32[64,1024]{1,0:T(8,128)} %param.14) | copy-start | bytes 786436
  82.1 66.9 %all-to-all-start.1 = ((f32[128,8,1024]{2,1,0:T(8,128)}), f32[128,8,1024]{2,1,0:T(8,128)}, u32[]{:S(2)}, u32[]{:S(2)}) async-start(f32[128,8,1024]{2,1,0:T(8,128)} %bitcast.14), calls=%async_computation.1 | async-start | bytes 8388608 | tf_op jit(solution)/shard_map/all_to_all | solution.py:47
  149.0 82.5 %all-to-all-start.3 = ((f32[128,1,8]{2,1,0:T(1,128)}), f32[128,1,8]{2,1,0:T(1,128)S(1)}, u32[]{:S(2)}, u32[]{:S(2)}) async-start(f32[128,1,8]{2,1,0:T(1,128)} %bitcast.7), calls=%async_computation.3 | async-start | bytes 131072 | tf_op jit(solution)/shard_map/all_to_all | solution.py:68
  231.5 277.3 %all-to-all-start.2 = ((f32[128,8,1024]{2,1,0:T(8,128)}), f32[128,8,1024]{2,1,0:T(8,128)}, u32[]{:S(2)}, u32[]{:S(2)}) async-start(f32[128,8,1024]{2,1,0:T(8,128)} %bitcast.15), calls=%async_computation.2 | async-start | bytes 8388608 | tf_op jit(solution)/shard_map/all_to_all | solution.py:67
  241.7 265.3 %all-reduce.3.cloned.1.call-start = ((), (), s32[]{:S(2)}) async-start(), calls=%async_computation.4 | async-start | bytes 524288 | tf_op jit(solution)/shard_map/psum | solution.py:87
Sparse Core Ops, SparseCore 0:
  368.1 138.9 all-reduce.2
where the time goes:
time: 528 us; the launch traced here: 527 us
  waiting for transfers between devices  125 us (24%)
  blocking collectives  117 us (22%)
  other arithmetic  115 us (22%)
  local copies, waits for them, and re-layouts  79.9 us (15%)
  starting transfers between devices  41.7 us (8%)
  matrix products  33.9 us (6%)
  between operations  14.2 us (3%)
    psum x1, waiting for transfers between devices, local(): off_sum, off_tot = lax.psum((off_part, off_cnt), ('src', 'rcv'))  125 us
    psum x1, blocking collectives, local(): off_sum, off_tot = lax.psum((off_part, off_cnt), ('src', 'rcv'))  104 us
    another operation x1, other arithmetic  34.8 us
    gather x2, local copies, waits for them, and re-layouts, local(): fetched[trace_slot]  23 us
    dot_general x1, matrix products, local(): spectra = jnp.dot(traces, table, preferred_element_type=jnp.float32)  21.9 us
    scatter-add x1, other arithmetic, local(): jax.ops.segment_sum(residual, trace_slot, num_segments=peers * slots)  21.2 us
    sub x1, other arithmetic, local(): logamp - source_terms[src_local] - fetched[trace_slot]  19.4 us
    gather x2, local copies, waits for them, and re-layouts, local(): source_terms[src_local]  19 us
  transfers between devices with their start and end apart: 5, of which 1 were waited for; matrix products, arithmetic and copies ran while one was open for 40% of the time, Pallas kernels for 0%

commit v1 on v0

v1 whole, which is shorter than its diff:
```python
import functools
import math

import jax
import jax.numpy as jnp
from jax import lax
from jax.experimental import pallas as pl
from jax.experimental.pallas import tpu as pltpu
from jax.sharding import PartitionSpec as P

NS = 2048
LANES = 128
ROWS = 1152
STEP = 2.0 * math.pi / NS
NT = (((1,), (1,)), ((), ()))


def trig_base(cb, sb):
    row = lax.broadcasted_iota(jnp.int32, (128, LANES), 0)
    col = lax.broadcasted_iota(jnp.int32, (128, LANES), 1)
    far = ((row * 16 * col) % NS).astype(jnp.float32) * STEP
    far_c, far_s = jnp.cos(far), jnp.sin(far)
    wide = (row * 16).astype(jnp.float32) * STEP
    wide_c, wide_s = jnp.cos(wide), jnp.sin(wide)
    row = lax.broadcasted_iota(jnp.int32, (16, LANES), 0)
    col = lax.broadcasted_iota(jnp.int32, (16, LANES), 1)
    near = ((row * col) % NS).astype(jnp.float32) * STEP
    near_c, near_s = jnp.cos(near), jnp.sin(near)
    half = (row.astype(jnp.float32) + 0.5) * STEP
    half_c, half_s = jnp.cos(half), jnp.sin(half)
    for b in range(128):
        fc, fs = far_c[b : b + 1], far_s[b : b + 1]
        wc, ws = wide_c[b : b + 1], wide_s[b : b + 1]
        taper = (0.5 - 0.5 * (wc * half_c - ws * half_s)) * (1.0 / math.sqrt(NS))
        cb[16 * b : 16 * b + 16, :] = taper * (fc * near_c - fs * near_s)
        sb[16 * b : 16 * b + 16, :] = taper * (fs * near_c + fc * near_s)


def chunk_table(c, rows, cb, sb, table):
    n = lax.broadcasted_iota(jnp.int32, (16, LANES), 0)
    turn = ((n * c) % 16).astype(jnp.float32) * (2.0 * math.pi / 16.0)
    tc, ts = jnp.cos(turn), jnp.sin(turn)
    for r in rows:
        bc, bs = cb[r : r + 16, :], sb[r : r + 16, :]
        table[r : r + 16, 0:LANES] = (bc * tc - bs * ts).astype(jnp.bfloat16)
        table[r : r + 16, LANES : 2 * LANES] = (-(bs * tc + bc * ts)).astype(jnp.bfloat16)


def split(x):
    upper = x.astype(jnp.bfloat16)
    return upper, (x - upper.astype(jnp.float32)).astype(jnp.bfloat16)


def local_kernel(idx, tr_hbm, src, off, sums, counts, tr, hot, table, cb, sb, low, sem):
    cp = pltpu.make_async_copy(tr_hbm, tr, sem)
    cp.start()
    trig_base(cb, sb)

    slot, first, second = idx[0:1, :], idx[1:2, :], idx[2:3, :]

    def hot_rows(i, _):
        r = pl.multiple_of(i * 32, 32)
        row = lax.broadcasted_iota(jnp.int32, (32, NS), 0) + r
        hit = (row == slot) | (row == first) | (row == second)
        hot[pl.ds(r, 32), 0:NS] = jnp.where(hit, 1.0, 0.0).astype(jnp.bfloat16)
        return 0

    lax.fori_loop(0, ROWS // 32, hot_rows, 0)
    cnt = lax.dot_general(hot[:, 0:NS], hot[1024:ROWS, 0:NS], NT, preferred_element_type=jnp.float32)
    counts[...] = cnt
    upper, lower = split(cnt)
    hot[:, NS : NS + LANES] = upper
    hot[:, NS + LANES : NS + 2 * LANES] = lower
    low[NS + 72 : NS + 128, :] = jnp.zeros((56, 2 * LANES), jnp.bfloat16)
    low[NS + 200 : NS + 256, :] = jnp.zeros((56, 2 * LANES), jnp.bfloat16)
    cp.wait()

    def chunk(c, _):
        lane = pl.multiple_of(c * LANES, LANES)
        chunk_table(c, range(0, NS, 16), cb, sb, table)
        for r in range(0, NS, 256):
            spec = jnp.dot(tr[r : r + 256, :], table[...], preferred_element_type=jnp.float32)
            re, im = spec[:, 0:LANES], spec[:, LANES:]
            amp = 0.5 * jnp.log(re * re + im * im + 0.01)
            upper, lower = split(amp)
            low[r : r + 256, 0:LANES] = upper
            low[r : r + 256, LANES:] = lower
        terms = jnp.concatenate([src[:, pl.ds(lane, LANES)], off[:, pl.ds(lane, LANES)]], axis=0)
        upper, lower = split(-terms)
        for r in (NS, NS + LANES):
            low[r : r + 72, 0:LANES] = upper
            low[r : r + 72, LANES:] = lower
        for r in range(0, ROWS, 384):
            out = jnp.dot(hot[r : r + 384, :], low[...], preferred_element_type=jnp.float32)
            sums[r : r + 384, pl.ds(lane, LANES)] = out[:, 0:LANES] + out[:, LANES:]
        return 0

    lax.fori_loop(0, 8, chunk, 0)


def local_sums(idx, traces, src, off):
    vmem = pl.BlockSpec(memory_space=pltpu.VMEM)
    return pl.pallas_call(
        local_kernel,
        out_shape=(
            jax.ShapeDtypeStruct((ROWS, 1024), jnp.float32),
            jax.ShapeDtypeStruct((ROWS, LANES), jnp.float32),
        ),
        in_specs=[vmem, pl.BlockSpec(memory_space=pl.ANY), vmem, vmem],
        out_specs=(vmem, vmem),
        scratch_shapes=[
            pltpu.VMEM((NS, NS), jnp.bfloat16),
            pltpu.VMEM((ROWS, NS + 256), jnp.bfloat16),
            pltpu.VMEM((NS, 256), jnp.bfloat16),
            pltpu.VMEM((NS, LANES), jnp.float32),
            pltpu.VMEM((NS, LANES), jnp.float32),
            pltpu.VMEM((NS + 256, 256), jnp.bfloat16),
            pltpu.SemaphoreType.DMA,
        ],
        compiler_params=pltpu.CompilerParams(vmem_limit_bytes=56 << 20),
        name="local_sums",
    )(idx, traces, src, off)


def local(traces, trace_source, trace_offset, trace_slot, request_list, src, rcv, off):
    axes = ("src", "rcv")
    s = lax.axis_index("src")
    first = trace_source - s * 8 + 1024
    idx = jnp.stack([trace_slot, first, trace_offset + 1032])
    idx = jnp.concatenate([idx, jnp.zeros((5, NS), jnp.int32)])
    sums, counts = local_sums(idx, traces, src, off)
    hi = lax.Precision.HIGHEST
    asked = lax.all_to_all(request_list.reshape(128, 8), axes, split_axis=0, concat_axis=0, tiled=True)
    got_cnt = lax.all_to_all(
        counts[:1024].reshape(128, 8, LANES), axes, split_axis=0, concat_axis=0, tiled=True
    ).reshape(1024, LANES)
    got = lax.all_to_all(
        sums[:1024].reshape(128, 8, 1024), axes, split_axis=0, concat_axis=0, tiled=True
    ).reshape(1024, 1024)
    dense = (asked.reshape(1, 1024) == jnp.arange(64)[:, None]).astype(jnp.float32)
    wide = jnp.tile(got_cnt[:, 0:8], (1, 32)) * (
        (jnp.arange(1024) // 32)[:, None] == (jnp.arange(256) // 8)[None, :]
    )
    n_src = jnp.dot(dense, wide, precision=hi)
    n_off = jnp.dot(dense, got_cnt[:, 8:72], precision=hi)
    tot = jnp.sum(n_off, axis=1)
    rsum = jnp.dot(dense, got, precision=hi)
    receiver_new = (rcv + rsum) / (tot + 1.0)[:, None]
    u_src = jnp.dot(n_src.T, rcv, precision=hi)
    u_off = jnp.dot(n_off.T, rcv, precision=hi)
    u_part = lax.psum_scatter(u_src, "src", scatter_dimension=0, tiled=True)
    src_sum, src_cnt = lax.psum((sums[1024:1032] - u_part, jnp.sum(counts[1024:1032, 8:72], axis=1)), "rcv")
    off_sum, off_cnt = lax.psum((sums[1032:1096] - u_off, jnp.sum(counts[1032:1096, 0:8], axis=1)), axes)
    source_new = src + src_sum / (src_cnt + 1.0)[:, None]
    offset_new = off + off_sum / (off_cnt + 1.0)[:, None]
    return (source_new, receiver_new, offset_new)


def solution(mesh):
    every = P(("src", "rcv"))
    return jax.shard_map(
        local,
        mesh=mesh,
        in_specs=(P(("src", "rcv"), None), every, every, every, P(("src", "rcv"), None, None), P("src", None), P(("src", "rcv"), None), P()),
        out_specs=(P("src", None), P(("src", "rcv"), None), P()),
        check_vma=False,
    )
```

time: 528 us -> 301 us (0.57)
  other arithmetic: 115 us -> 8.58 us
  local copies, waits for them, and re-layouts: 79.9 us -> 9.01 us
  waiting for transfers between devices: 125 us -> 78.2 us
  Pallas kernels: 0 us -> 39.8 us
  matrix products: 33.9 us -> 10.2 us
  starting transfers between devices: 41.7 us -> 26.1 us
  blocking collectives: 117 us -> 110 us
    gather x7 -> x0, local copies, waits for them, and re-layouts: 66.4 us -> none  [the longest x2 23 us: local(): fetched[trace_slot]]
    psum x1, waiting for transfers between devices: 125 us -> 68.8 us  [local(): lax.psum((sums[1032:1096] - u_off, jnp.sum(counts[1032:1096, 0:8], axis=1...]
    scatter-add x4 -> x0, other arithmetic: 53.9 us -> none  [the longest x1 21.2 us: local(): jax.ops.segment_sum(residual, trace_slot, num_segments=peers * slots)]
    pallas_call x0 -> x1, Pallas kernels: none -> 39.8 us  [local_sums(): pl.pallas_call(local_kernel, out_shape=(jax.ShapeDtypeStruct((ROWS, 1024)...]
    another operation x1 -> x0, other arithmetic: 34.8 us -> none
    dot_general x3 -> x5, matrix products: 33.9 us -> 10.2 us  [the longest x1 4.62 us: local(): rsum = jnp.dot(dense, got, precision=hi)]
    sub x1, other arithmetic: 19.4 us -> 0.78 us  [local(): sums[1024:1032] - u_part]
    all_to_all x4 -> x3, starting transfers between devices: 41.7 us -> 26.1 us  [the longest x1 11.5 us: local(): lax.all_to_all(request_list.reshape(128, 8), axes, split_axis=0, concat_a...]
  transfers between devices with their start and end apart: 5 -> 5, of which waited for: 1 -> 2; matrix products, arithmetic and copies ran while one was open for 40% -> 7% of each run, Pallas kernels for 0% -> 13%
where the time goes in v1:
time: 301 us; the launch traced here: 297 us
  blocking collectives  110 us (37%)
  waiting for transfers between devices  78.2 us (26%)
  Pallas kernels  39.8 us (13%)
  starting transfers between devices  26.1 us (9%)
  between operations  15.6 us (5%)
  matrix products  10.2 us (3%)
  local copies, waits for them, and re-layouts  9.01 us (3%)
  other arithmetic  8.58 us (3%)
    psum x1, blocking collectives, local(): lax.psum((sums[1032:1096] - u_off, jnp.sum(counts[1032:1096, 0:8], axis=1...  97.1 us
    psum x1, waiting for transfers between devices, local(): lax.psum((sums[1032:1096] - u_off, jnp.sum(counts[1032:1096, 0:8], axis=1...  68.8 us
    pallas_call x1, Pallas kernels, local_sums(): pl.pallas_call(local_kernel, out_shape=(jax.ShapeDtypeStruct((ROWS, 1024)...  39.8 us
    psum x1, blocking collectives, local(): lax.psum((sums[1024:1032] - u_part, jnp.sum(counts[1024:1032, 8:72], axis...  12.7 us
    all_to_all x1, starting transfers between devices, local(): lax.all_to_all(request_list.reshape(128, 8), axes, split_axis=0, concat_a...  11.5 us
    all_to_all x1, starting transfers between devices, local(): lax.all_to_all(counts[:1024].reshape(128, 8, LANES), axes, split_axis=0,...  9.78 us
    all_to_all x1, waiting for transfers between devices, local(): lax.all_to_all(counts[:1024].reshape(128, 8, LANES), axes, split_axis=0,...  9.34 us
  transfers between devices with their start and end apart: 5, of which 2 were waited for; matrix products, arithmetic and copies ran while one was open for 7% of the time, Pallas kernels for 13%

profile of v1, /device:TPU:1, one launch (start us, length us, event | category | flops | bytes accessed | tf_op | source)
XLA Modules:
  0.0 297.3 jit_solution(17468395623145028337)
XLA Ops:
  8.0 1.4 copy.13
  9.4 11.5 %all-to-all-start = ((s32[128,1,8]{2,1,0:T(1,128)}), s32[128,1,8]{2,1,0:T(1,128)S(1)}, u32[]{:S(2)}, u32[]{:S(2)}) async-start(s32[128,1,8]{2,1,0:T(1,128)} %bitcast.3), calls=%async_computation | async-start | bytes 131072 | tf_op jit(solution)/shard_map/all_to_all | solution.py:133
  20.9 0.7 broadcast_add_fusion
  21.6 0.1 pad.3.clone
  21.7 0.7 subtract_add_fusion
  22.4 1.4 add_add_fusion.idx
  23.8 39.8 %local_sums.1 = (f32[1152,1024]{1,0:T(8,128)}, f32[1152,128]{1,0:T(8,128)}) custom-call(s32[8,2048]{1,0:T(8,128)} %add_add_fusion.idx, bf16[2048,2048]{1,0:T(8,128)(2,1)} %tr_hbm.1, f32[8,1024]{1,0:T(8,128)} %src.1, f32[64,1024]{1,0:T(8,128)} %off.1), custom_call_target="tpu_custom_call" | custom-call | tf_op jit(solution)/shard_map/local_sums/pallas_call | solution.py:103
  63.7 1.9 slice_bitcast_fusion.1
  65.6 0.0 all-to-all-done
  65.6 9.8 %all-to-all-start.1 = ((f32[128,8,128]{2,1,0:T(8,128)}), f32[128,8,128]{2,1,0:T(8,128)S(1)}, u32[]{:S(2)}, u32[]{:S(2)}) async-start(f32[128,8,128]{2,1,0:T(8,128)} %slice_bitcast_fusion.1), calls=%async_computation.1 | async-start | bytes 1048576 | tf_op jit(solution)/shard_map/all_to_all | solution.py:134
  75.4 4.8 %slice_bitcast_fusion = f32[128,8,1024]{2,1,0:T(8,128)} fusion(f32[1152,1024]{1,0:T(8,128)} %get-tuple-element.5), kind=kLoop, calls=%fused_computation.2 | loop fusion | bytes 8388608 | tf_op jit(solution)/shard_map/reshape | solution.py:138
  80.2 0.0 copy-start
  80.2 9.3 %all-to-all-done.1 = f32[128,8,128]{2,1,0:T(8,128)S(1)} async-done(((f32[128,8,128]{2,1,0:T(8,128)}), f32[128,8,128]{2,1,0:T(8,128)S(1)}, u32[]{:S(2)}, u32[]{:S(2)}) %all-to-all-start.1) | async-done | bytes 524320 | tf_op jit(solution)/shard_map/all_to_all | solution.py:134
  89.5 4.8 %all-to-all-start.2 = ((f32[128,8,1024]{2,1,0:T(8,128)}), f32[128,8,1024]{2,1,0:T(8,128)}, u32[]{:S(2)}, u32[]{:S(2)}) async-start(f32[128,8,1024]{2,1,0:T(8,128)} %slice_bitcast_fusion), calls=%async_computation.3 | async-start | bytes 8388608 | tf_op jit(solution)/shard_map/all_to_all | solution.py:137
  94.3 0.0 copy-start.1
  94.3 0.0 copy-start.2
  94.3 0.0 all-reduce.3.cloned.1.call-start
  94.4 0.5 broadcast.91
  94.9 0.8 reduce.3
  95.7 0.1 eq.28
  95.8 0.2 copy.15
  96.0 0.8 fusion.23
  96.7 0.0 copy-done
  96.8 2.0 convolution_subtract_fusion
  98.8 0.0 all-reduce.3.cloned.1.call-update
  98.8 0.0 reduce-scatter.2.cloned.1.call-start
  98.8 0.8 fusion.8
  99.6 2.0 fusion.24
  101.7 0.0 reduce-scatter.2.cloned.1.call-update
  101.7 0.9 slice_reduce_fusion
  102.6 97.1 %psum.31 = f32[64]{0:T(128)S(1)} all-reduce(f32[64]{0:T(128)S(1)} %slice_reduce_fusion), channel_id=1, replica_groups=mesh['src'=32,'rcv'=4] {'src','rcv'}, use_global_device_ids=true, to_apply=%region_7.8 | all-reduce | flops 64 | bytes 512 | tf_op jit(solution)/shard_map/psum | solution.py:153
  199.6 0.9 slice_reduce_fusion.1
  200.5 68.8 %all-reduce.3.cloned.1.call-done = f32[64,1024]{1,0:T(8,128)} async-done(((f32[64,1024]{1,0:T(8,128)}), f32[64,1024]{1,0:T(8,128)}) %all-reduce.3.cloned.1.call-update) | async-done | bytes 262160 | tf_op jit(solution)/shard_map/psum | solution.py:153
  269.3 0.0 copy-done.1
  269.3 1.8 divide_add_fusion
  271.0 0.0 reduce-scatter.2.cloned.1.call-done
  271.0 0.8 slice_subtract_fusion
  271.8 12.7 %all-reduce = (f32[8,1024]{1,0:T(8,128)S(1)}, f32[8]{0:T(128)S(1)}) all-reduce(f32[8,1024]{1,0:T(8,128)S(1)} %slice_subtract_fusion, f32[8]{0:T(128)S(1)} %slice_reduce_fusion.1), channel_id=1, replica_groups=mesh['src'=32,'rcv'=4] {'rcv'}, use_global_device_ids=true, to_apply=%region_1.2 | all-reduce | flops 8200 | bytes 65600 | tf_op jit(solution)/shard_map/psum | solution.py:152
  284.5 0.0 copy-done.2
  284.5 0.7 divide_add_fusion.1
  285.2 0.0 all-to-all-done.2
  285.2 4.6 %fusion.5 = f32[64,1024]{1,0:T(8,128)} fusion(f32[64,1024]{1,0:T(8,128)S(1)} %copy-done, f32[128,8,1024]{2,1,0:T(8,128)} %all-to-all-done.2, f32[64]{0:T(128)S(1)} %broadcast_add_fusion.2, s32[1024]{0:T(1024)S(1)} %eq.28), kind=kOutput, calls=%fused_computation.5 | convolution fusion | flops 805502976 | bytes 4722944 | tf_op jit(solution)/shard_map/dot_general | solution.py:147
  (6 shorter events, 0.0 us)
Async XLA Ops:
  9.4 56.2 %all-to-all-start = ((s32[128,1,8]{2,1,0:T(1,128)}), s32[128,1,8]{2,1,0:T(1,128)S(1)}, u32[]{:S(2)}, u32[]{:S(2)}) async-start(s32[128,1,8]{2,1,0:T(1,128)} %bitcast.3), calls=%async_computation | async-start | bytes 131072 | tf_op jit(solution)/shard_map/all_to_all | solution.py:133
  65.6 23.9 %all-to-all-start.1 = ((f32[128,8,128]{2,1,0:T(8,128)}), f32[128,8,128]{2,1,0:T(8,128)S(1)}, u32[]{:S(2)}, u32[]{:S(2)}) async-start(f32[128,8,128]{2,1,0:T(8,128)} %slice_bitcast_fusion.1), calls=%async_computation.1 | async-start | bytes 1048576 | tf_op jit(solution)/shard_map/all_to_all | solution.py:134
  80.2 16.6 %copy-start = (f32[64,1024]{1,0:T(8,128)S(1)}, f32[64,1024]{1,0:T(8,128)}, u32[]{:S(2)}) copy-start(f32[64,1024]{1,0:T(8,128)} %param.14) | copy-start | bytes 786436
  89.5 195.7 %all-to-all-start.2 = ((f32[128,8,1024]{2,1,0:T(8,128)}), f32[128,8,1024]{2,1,0:T(8,128)}, u32[]{:S(2)}, u32[]{:S(2)}) async-start(f32[128,8,1024]{2,1,0:T(8,128)} %slice_bitcast_fusion), calls=%async_computation.3 | async-start | bytes 8388608 | tf_op jit(solution)/shard_map/all_to_all | solution.py:137
  94.3 175.0 %copy-start.1 = (f32[64,1024]{1,0:T(8,128)S(1)}, f32[64,1024]{1,0:T(8,128)}, u32[]{:S(2)}) copy-start(f32[64,1024]{1,0:T(8,128)} %off.1) | copy-start | bytes 786436
  94.3 190.2 %copy-start.2 = (f32[8,1024]{1,0:T(8,128)S(1)}, f32[8,1024]{1,0:T(8,128)}, u32[]{:S(2)}) copy-start(f32[8,1024]{1,0:T(8,128)} %src.1) | copy-start | bytes 98308
  94.3 174.9 %all-reduce.3.cloned.1.call-start = ((), (), s32[]{:S(2)}) async-start(), calls=%async_computation.5 | async-start | bytes 524288 | tf_op jit(solution)/shard_map/psum | solution.py:153
  98.8 172.3 %reduce-scatter.2.cloned.1.call-start = ((), (), s32[]{:S(2)}) async-start(), calls=%async_computation.4 | async-start | bytes 1081344 | tf_op jit(solution)/shard_map/reduce_scatter | solution.py:151
Sparse Core Ops, SparseCore 0:
  101.2 168.0 all-reduce.2
Sparse Core Ops, SparseCore 1:
  102.8 77.8 reduce-scatter.1

commit v2 on v1

v2 whole, which is shorter than its diff:
```python
import math

import jax
import jax.numpy as jnp
from jax import lax
from jax.experimental import pallas as pl
from jax.experimental.pallas import tpu as pltpu
from jax.sharding import PartitionSpec as P

NS = 2048
LANES = 128
ROWS = 1152
WIDE = 1024 + LANES
MESH = pl.DeviceIdType.MESH
KINDS = (0, 1, 2, 0, 1, 2, 0, 1)
SECOND = ("y", "z", "x")
THIRD = ("z", "x", "y")
TN = (((0,), (0,)), ((), ()))
STEP = 2.0 * math.pi / NS
NT = (((1,), (1,)), ((), ()))


def trig_base(cb, sb):
    row = lax.broadcasted_iota(jnp.int32, (128, LANES), 0)
    col = lax.broadcasted_iota(jnp.int32, (128, LANES), 1)
    far = ((row * 16 * col) % NS).astype(jnp.float32) * STEP
    far_c, far_s = jnp.cos(far), jnp.sin(far)
    wide = (row * 16).astype(jnp.float32) * STEP
    wide_c, wide_s = jnp.cos(wide), jnp.sin(wide)
    row = lax.broadcasted_iota(jnp.int32, (16, LANES), 0)
    col = lax.broadcasted_iota(jnp.int32, (16, LANES), 1)
    near = ((row * col) % NS).astype(jnp.float32) * STEP
    near_c, near_s = jnp.cos(near), jnp.sin(near)
    half = (row.astype(jnp.float32) + 0.5) * STEP
    half_c, half_s = jnp.cos(half), jnp.sin(half)
    for b in range(128):
        fc, fs = far_c[b : b + 1], far_s[b : b + 1]
        wc, ws = wide_c[b : b + 1], wide_s[b : b + 1]
        taper = (0.5 - 0.5 * (wc * half_c - ws * half_s)) * (1.0 / math.sqrt(NS))
        cb[16 * b : 16 * b + 16, :] = taper * (fc * near_c - fs * near_s)
        sb[16 * b : 16 * b + 16, :] = taper * (fs * near_c + fc * near_s)


def chunk_table(c, rows, cb, sb, table):
    n = lax.broadcasted_iota(jnp.int32, (16, LANES), 0)
    turn = ((n * c) % 16).astype(jnp.float32) * (2.0 * math.pi / 16.0)
    tc, ts = jnp.cos(turn), jnp.sin(turn)
    for r in rows:
        bc, bs = cb[r : r + 16, :], sb[r : r + 16, :]
        table[r : r + 16, 0:LANES] = (bc * tc - bs * ts).astype(jnp.bfloat16)
        table[r : r + 16, LANES : 2 * LANES] = (-(bs * tc + bc * ts)).astype(jnp.bfloat16)


def split(x):
    upper = x.astype(jnp.bfloat16)
    return upper, (x - upper.astype(jnp.float32)).astype(jnp.bfloat16)


def kernel(
    tr_hbm, slot_ref, src_ref, off_ref, list_ref, s_ref, r_ref, o_ref,
    snew, rnew, onew,
    tr, hot, table, cb, sb, low, extra,
    grid, b1, b1d, b2, b2d, b3, pick,
    c2, c3, us, e0, e1, v2, e2, uoff,
    ex, off, eo, ho, eh, eh2, eh3, fa, inv,
    tr_sem, s0s, s0r, s1s, s1r, s2s, s2r, s3s, s3r, us_s, us_r, os_s, os_r, xs_s, xs_r,
):
    f32, bf16 = jnp.float32, jnp.bfloat16
    group, x = lax.axis_index("src"), lax.axis_index("rcv")
    c, z, y = lax.rem(group, 2), lax.rem(group // 2, 4), group // 8
    me = {"x": x, "y": y, "z": z}

    def at(ax, k, flip=False):
        p = dict(me)
        if ax:
            p[ax] = lax.rem(p[ax] + k, 4)
        core = 1 - c if flip else c
        return ((p["y"] * 4 + p["z"]) * 2 + core, p["x"])

    def step(ax, k):
        return lax.rem(me[ax] + k, 4)

    twin = at(None, 0, True)
    peers = [twin] + [at(ax, k) for ax in "xyz" for k in (1, 2, 3)] + [at("x", k, True) for k in (1, 2, 3)]
    barrier = pltpu.get_barrier_semaphore()
    for p in peers:
        pl.semaphore_signal(barrier, inc=1, device_id=p, device_id_type=MESH)

    load = pltpu.make_async_copy(tr_hbm, tr, tr_sem)
    load.start()

    def rc(a, b, ss, rs, dev):
        return pltpu.make_async_remote_copy(
            src_ref=a, dst_ref=b, send_sem=ss, recv_sem=rs, device_id=dev, device_id_type=MESH
        )

    def start(copies):
        for cp in copies:
            cp.start()

    def wait(copies):
        for cp in copies:
            cp.wait()

    def x0(i):
        return [rc(grid.at[i, 2], grid.at[i, 1], s0s.at[i], s0r.at[i], twin)]

    def x1(i, kind, n):
        out = []
        for k in (1, 2, 3):
            j = step("xyz"[kind], k)
            part = (grid.at[i, 0:2, :, :, j], grid.at[i, 0:2, j], grid.at[i, 0:2, :, j])[kind]
            out.append(rc(part, b1.at[n, k - 1], s1s.at[n, k - 1], s1r.at[n, k - 1], at("xyz"[kind], k)))
        return out

    def x2(i, kind):
        ax = SECOND[kind]
        return [
            rc(b1d.at[i, step(ax, k)], b2.at[i, k - 1], s2s.at[i, k - 1], s2r.at[i, k - 1], at(ax, k))
            for k in (1, 2, 3)
        ]

    def x3(i, kind):
        ax = THIRD[kind]
        return [
            rc(b2d.at[i, step(ax, k)], b3.at[i, k - 1], s3s.at[i, k - 1], s3r.at[i, k - 1], at(ax, k))
            for k in (1, 2, 3)
        ]

    def c_x2():
        return [
            rc(b1d.at[8, step("y", k)], c2.at[k], s2s.at[8, k - 1], s2r.at[8, k - 1], at("y", k)) for k in (1, 2, 3)
        ]

    def c_x3():
        return [
            rc(c2.at[:, step("z", k)], c3.at[k - 1], s3s.at[8, k - 1], s3r.at[8, k - 1], at("z", k)) for k in (1, 2, 3)
        ]

    def u_core():
        return [rc(us.at[1], e0, us_s.at[0], us_r.at[0], twin)]

    def u_y():
        return [rc(us.at[0, :, k], e1.at[k - 1], us_s.at[k], us_r.at[k], at("y", 4 - k)) for k in (1, 2, 3)]

    def u_z():
        return [rc(v2.at[k], e2.at[k - 1], us_s.at[3 + k], us_r.at[3 + k], at("z", 4 - k)) for k in (1, 2, 3)]

    def src_x():
        return [rc(ex.at[x], ex.at[x], xs_s.at[k - 1], xs_r.at[k - 1], at("x", k)) for k in (1, 2, 3)]

    def off_core():
        return [rc(off.at[1 - c], eo, os_s.at[0], os_r.at[0], twin)]

    def off_x():
        return [rc(ho.at[step("x", k)], eh.at[k - 1], os_s.at[k], os_r.at[k], at("x", k)) for k in (1, 2, 3)]

    def off_y():
        return [rc(eh2.at[y], eh2.at[y], os_s.at[3 + k], os_r.at[3 + k], at("y", k)) for k in (1, 2, 3)]

    def off_z():
        return [rc(eh3.at[z], eh3.at[z], os_s.at[6 + k], os_r.at[6 + k], at("z", k)) for k in (1, 2, 3)]

    def off_all():
        to = [at("x", k) for k in (1, 2, 3)] + [twin] + [at("x", k, True) for k in (1, 2, 3)]
        return [rc(fa.at[c, x], fa.at[c, x], os_s.at[10 + n], os_r.at[10 + n], d) for n, d in enumerate(to)]

    s = slot_ref[...]
    row_of = (
        (((s >> 5) & 1) ^ c) * 512 + (s >> 8) * 128 + ((s >> 6) & 3) * 32 + ((s >> 3) & 3) * 8 + (s & 7)
    )
    first = src_ref[...] - group * 8 + 1024
    second = off_ref[...] + 1032

    def hot_rows(i, _):
        r = pl.multiple_of(i * 32, 32)
        row = lax.broadcasted_iota(jnp.int32, (32, LANES), 0) + r
        for b in range(16):
            hit = row == row_of[b : b + 1, :]
            hot[pl.ds(r, 32), b * LANES : (b + 1) * LANES] = jnp.where(hit, 1.0, 0.0).astype(bf16)
        return 0

    lax.fori_loop(0, 32, hot_rows, 0)
    for r in range(1024, ROWS, 32):
        row = lax.broadcasted_iota(jnp.int32, (32, LANES), 0) + r
        for b in range(16):
            hit = (row == first[b : b + 1, :]) | (row == second[b : b + 1, :])
            hot[r : r + 32, b * LANES : (b + 1) * LANES] = jnp.where(hit, 1.0, 0.0).astype(bf16)

    cnt = lax.dot_general(hot[:, 0:NS], hot[1024:ROWS, 0:NS], NT, preferred_element_type=f32)
    upper, lower = split(cnt)
    hot[:, NS : NS + LANES] = upper
    hot[:, NS + LANES : NS + 2 * LANES] = lower
    low[NS + 72 : NS + 128, :] = jnp.zeros((56, 2 * LANES), bf16)
    low[NS + 200 : NS + 256, :] = jnp.zeros((56, 2 * LANES), bf16)
    lane = lax.broadcasted_iota(jnp.int32, (1, LANES), 1)
    count_s = jnp.sum(jnp.where((lane >= 8) & (lane < 72), cnt[1024:1032], 0.0), axis=1, keepdims=True)
    count_o = jnp.sum(jnp.where(lane < 8, cnt[1032:1096], 0.0), axis=1, keepdims=True)
    extra[0:8, 1024:WIDE] = jnp.broadcast_to(count_s, (8, LANES))
    extra[8:72, 1024:WIDE] = jnp.broadcast_to(count_o, (64, LANES))

    asked = list_ref[...].astype(f32)
    for yy in range(4):
        for zz in range(4):
            for xx in range(4):
                p = (yy * 4 + zz) * 8 + xx
                even = jnp.broadcast_to(asked[:, p : p + 1], (8, LANES))
                odd = jnp.broadcast_to(asked[:, p + 4 : p + 5], (8, LANES))
                own, far = jnp.where(c == 0, even, odd), jnp.where(c == 0, odd, even)
                r = ((yy * 4 + zz) * 4 + xx) * 8
                grid[8, 0, yy, zz, xx] = jnp.where(lane == 80 + 8, own, cnt[r : r + 8])
                q = cnt[512 + r : 520 + r]
                moved = jnp.where((lane >= 80) & (lane < 88), pltpu.roll(q, 80, 1), jnp.where(lane < 8, 0.0, q))
                grid[8, 2, yy, zz, xx] = jnp.where(lane == 80 + 8, far, moved)

    pl.semaphore_wait(barrier, len(peers))
    start(x0(8))
    trig_base(cb, sb)
    load.wait()

    def rows64(i, n, kind, p, q):
        own = (
            grid[i, 0:2, p, q, x] if kind == 0 else grid[i, 0:2, y, p, q] if kind == 1 else grid[i, 0:2, p, z, q]
        )
        return jnp.concatenate([own.reshape(16, LANES), b1[n, :, :, p, q].reshape(48, LANES)], axis=0)

    def densify(i, n, kind):
        def one(m, _):
            p, q = m // 4, lax.rem(m, 4)
            upper, lower = split(rows64(i, n, kind, p, q))
            both = jnp.concatenate([upper, lower], axis=1)
            out = jnp.dot(pick[kind, m], both, preferred_element_type=f32)
            total = out[:, 0:LANES] + out[:, LANES:]
            if kind == 2:
                b1d[i, q, p] = total
            else:
                b1d[i, p, q] = total
            return 0

        lax.fori_loop(0, 16, one, 0, unroll=4)

    def counts_1():
        wait(x0(8))
        for kind in range(3):
            start(x1(8, kind, 8 + kind))

    def counts_2():
        eye = jnp.where(
            lax.broadcasted_iota(jnp.int32, (64, 64), 0) == lax.broadcasted_iota(jnp.int32, (64, 64), 1), 1.0, 0.0
        ).astype(bf16)
        col = lax.broadcasted_iota(jnp.int32, (64, 64), 1).astype(f32)
        for kind in range(3):
            wait(x1(8, kind, 8 + kind))

            def one(m, _, kind=kind):
                rows = rows64(8, 8 + kind, kind, m // 4, lax.rem(m, 4))
                flipped = jnp.where(rows[:, 88:89] == col, 1.0, 0.0).astype(bf16)
                pick[kind, m] = lax.dot_general(eye, flipped, NT, preferred_element_type=f32).astype(bf16)
                return 0

            lax.fori_loop(0, 16, one, 0, unroll=4)
        densify(8, 8, 0)
        start(c_x2())

    def counts_3():
        wait(c_x2())
        c2[0] = b1d[8, y]
        start(c_x3())

    def counts_4():
        wait(c_x3())
        total = jnp.zeros((64, LANES), f32)
        w0, w1 = total, total
        for kz in range(4):
            for ky in range(4):
                mm = c2[ky, z] if kz == 0 else c3[kz - 1, ky]
                n = 8 * (kz * 4 + ky)
                total = total + mm
                a = jnp.where(lane < 8, mm, 0.0)
                b = jnp.where((lane >= 80) & (lane < 88), mm, 0.0)
                w0 = w0 + (pltpu.roll(a, n, 1) if n else a)
                w1 = w1 + pltpu.roll(b, (n + 48) % 128, 1)
        offs = jnp.where((lane >= 8) & (lane < 72), total, 0.0)
        hits = jnp.sum(offs, axis=1, keepdims=True)
        inv[...] = jnp.broadcast_to(1.0 / (hits + 1.0), (64, LANES))
        wide = jnp.concatenate([w0, w1, pltpu.roll(offs, 120, 1)], axis=1)
        upper, lower = split(wide)
        left = jnp.concatenate([upper, lower], axis=0)
        for h in range(4):
            r1, r2 = split(r_ref[:, h * 256 : h * 256 + 256])
            both = jnp.concatenate([r1, r2], axis=1)
            out = lax.dot_general(left, jnp.concatenate([both, both], axis=0), TN, preferred_element_type=f32)
            u = out[:, 0:256] + out[:, 256:]
            us[:, :, :, :, h * 256 : h * 256 + 256] = u[0:256].reshape(2, 4, 4, 8, 256)
            uoff[:, h * 256 : h * 256 + 256] = u[256:320]
        start(u_core())

    def counts_5():
        wait(u_core())
        us[0] = us[0] + e0[...]
        start(u_y())

    def counts_6():
        wait(u_y())
        v2[...] = us[0, :, 0] + e1[0] + e1[1] + e1[2]
        start(u_z())

    def counts_7():
        wait(u_z())

    def w0(i):
        wait(x0(i))
        start(x1(i, KINDS[i], i))

    def w1(i):
        wait(x1(i, KINDS[i], i))
        densify(i, i, KINDS[i])
        start(x2(i, KINDS[i]))

    def w2(i):
        wait(x2(i, KINDS[i]))
        b2d[i] = b1d[i, me[SECOND[KINDS[i]]]] + b2[i, 0] + b2[i, 1] + b2[i, 2]
        start(x3(i, KINDS[i]))

    def w3(i):
        wait(x3(i, KINDS[i]))
        total = b2d[i, me[THIRD[KINDS[i]]]] + b3[i, 0] + b3[i, 1] + b3[i, 2]
        cols = slice(i * LANES, (i + 1) * LANES)
        rnew[:, cols] = (r_ref[:, cols] + total) * inv[...]

    mid = {0: [counts_1], 1: [lambda: w0(0)], 2: [lambda: w0(1), counts_3], 3: [lambda: w0(2), counts_4],
           4: [lambda: w0(3), counts_5], 5: [lambda: w0(4), counts_6], 6: [lambda: w0(5), counts_7], 7: [lambda: w0(6)]}
    end = {1: [counts_2], 3: [lambda: w1(0)], 4: [lambda: w1(1)], 5: [lambda: w1(2), lambda: w2(0)],
           6: [lambda: w1(3), lambda: w2(1)], 7: [lambda: w1(4), lambda: w2(2), lambda: w3(0)]}

    def chunk(i, _):
        at_lane = pl.multiple_of(i * LANES, LANES)
        chunk_table(i, range(0, NS, 16), cb, sb, table)
        for r in range(0, NS, 256):
            spec = jnp.dot(tr[r : r + 256, :], table[...], preferred_element_type=f32)
            re, im = spec[:, 0:LANES], spec[:, LANES:]
            amp = 0.5 * jnp.log(re * re + im * im + 0.01)
            upper, lower = split(amp)
            low[r : r + 256, 0:LANES] = upper
            low[r : r + 256, LANES:] = lower
        terms = jnp.concatenate([s_ref[:, pl.ds(at_lane, LANES)], o_ref[:, pl.ds(at_lane, LANES)]], axis=0)
        upper, lower = split(-terms)
        for r in (NS, NS + LANES):
            low[r : r + 72, 0:LANES] = upper
            low[r : r + 72, LANES:] = lower
        for n, todo in mid.items():
            @pl.when(i == n)
            def _(todo=todo):
                for f in todo:
                    f()
        for half in (0, 1):
            out = jnp.dot(hot[half * 512 : half * 512 + 512, :], low[...], preferred_element_type=f32)
            grid[i, 2 * half] = (out[:, 0:LANES] + out[:, LANES:]).reshape(4, 4, 4, 8, LANES)
        out = jnp.dot(hot[1024:ROWS, :], low[...], preferred_element_type=f32)
        extra[:, pl.ds(at_lane, LANES)] = (out[:, 0:LANES] + out[:, LANES:])[0:72]
        for n in range(8):
            @pl.when(i == n)
            def _(n=n):
                start(x0(n))
                for f in end.get(n, []):
                    f()
        return 0

    lax.fori_loop(0, 8, chunk, 0)

    ex[x, :, 0:1024] = extra[0:8, 0:1024] - (v2[0] + e2[0] + e2[1] + e2[2])
    ex[x, :, 1024:WIDE] = extra[0:8, 1024:WIDE]
    start(src_x())
    off[:, :, :, 0:1024] = (extra[8:72, 0:1024] - uoff[...]).reshape(2, 4, 8, 1024)
    off[:, :, :, 1024:WIDE] = extra[8:72, 1024:WIDE].reshape(2, 4, 8, LANES)
    start(off_core())
    w0(7)
    wait(off_core())
    ho[...] = off[c] + eo[...]
    start(off_x())
    w1(5)
    w2(3)
    w3(1)
    wait(off_x())
    eh2[y] = ho[x] + eh[0] + eh[1] + eh[2]
    start(off_y())
    w1(6)
    w2(4)
    w3(2)
    wait(off_y())
    eh3[z] = eh2[0] + eh2[1] + eh2[2] + eh2[3]
    start(off_z())
    w1(7)
    w2(5)
    w3(3)
    wait(off_z())
    fa[c, x] = eh3[0] + eh3[1] + eh3[2] + eh3[3]
    start(off_all())
    w2(6)
    w3(4)
    w2(7)
    w3(5)
    wait(src_x())
    total = ex[0] + ex[1] + ex[2] + ex[3]
    snew[...] = s_ref[...] + total[:, 0:1024] / (total[:, 1024:1025] + 1.0)
    wait(off_all())
    total = fa[...].reshape(64, WIDE)
    onew[...] = o_ref[...] + total[:, 0:1024] / (total[:, 1024:1025] + 1.0)
    w3(6)
    w3(7)


def local(traces, trace_source, trace_offset, trace_slot, request_list, src, rcv, off):
    f32, bf16 = jnp.float32, jnp.bfloat16
    vmem = pl.BlockSpec(memory_space=pltpu.VMEM)
    dma = pltpu.SemaphoreType.DMA
    scratch = [
        pltpu.VMEM((NS, NS), bf16),
        pltpu.VMEM((ROWS, NS + 256), bf16),
        pltpu.VMEM((NS, 256), bf16),
        pltpu.VMEM((NS, LANES), f32),
        pltpu.VMEM((NS, LANES), f32),
        pltpu.VMEM((NS + 256, 256), bf16),
        pltpu.VMEM((72, WIDE), f32),
        pltpu.VMEM((9, 3, 4, 4, 4, 8, LANES), f32),
        pltpu.VMEM((11, 3, 2, 4, 4, 8, LANES), f32),
        pltpu.VMEM((9, 4, 4, 64, LANES), f32),
        pltpu.VMEM((8, 3, 4, 64, LANES), f32),
        pltpu.VMEM((8, 4, 64, LANES), f32),
        pltpu.VMEM((8, 3, 64, LANES), f32),
        pltpu.VMEM((3, 16, 64, 64), bf16),
        pltpu.VMEM((4, 4, 64, LANES), f32),
        pltpu.VMEM((3, 4, 64, LANES), f32),
        pltpu.VMEM((2, 4, 4, 8, 1024), f32),
        pltpu.VMEM((4, 4, 8, 1024), f32),
        pltpu.VMEM((3, 4, 8, 1024), f32),
        pltpu.VMEM((4, 8, 1024), f32),
        pltpu.VMEM((3, 8, 1024), f32),
        pltpu.VMEM((64, 1024), f32),
        pltpu.VMEM((4, 8, WIDE), f32),
        pltpu.VMEM((2, 4, 8, WIDE), f32),
        pltpu.VMEM((4, 8, WIDE), f32),
        pltpu.VMEM((4, 8, WIDE), f32),
        pltpu.VMEM((3, 8, WIDE), f32),
        pltpu.VMEM((4, 8, WIDE), f32),
        pltpu.VMEM((4, 8, WIDE), f32),
        pltpu.VMEM((2, 4, 8, WIDE), f32),
        pltpu.VMEM((64, LANES), f32),
        dma,
        dma((9,)), dma((9,)), dma((11, 3)), dma((11, 3)), dma((9, 3)), dma((9, 3)), dma((9, 3)), dma((9, 3)),
        dma((7,)), dma((7,)), dma((17,)), dma((17,)), dma((3,)), dma((3,)),
    ]
    return pl.pallas_call(
        kernel,
        out_shape=(
            jax.ShapeDtypeStruct(src.shape, f32),
            jax.ShapeDtypeStruct(rcv.shape, f32),
            jax.ShapeDtypeStruct(off.shape, f32),
        ),
        in_specs=[pl.BlockSpec(memory_space=pl.ANY)] + [vmem] * 7,
        out_specs=(vmem, vmem, vmem),
        scratch_shapes=scratch,
        compiler_params=pltpu.CompilerParams(vmem_limit_bytes=58 << 20, collective_id=0, has_side_effects=True),
        name="update",
    )(
        traces,
        trace_slot.reshape(16, LANES),
        trace_source.reshape(16, LANES),
        trace_offset.reshape(16, LANES),
        request_list.reshape(128, 8).T,
        src,
        rcv,
        off,
    )


def solution(mesh):
    every = P(("src", "rcv"))
    return jax.shard_map(
        local,
        mesh=mesh,
        in_specs=(P(("src", "rcv"), None), every, every, every, P(("src", "rcv"), None, None), P("src", None), P(("src", "rcv"), None), P()),
        out_specs=(P("src", None), P(("src", "rcv"), None), P()),
        check_vma=False,
    )
```

time: 301 us -> 106 us (0.35)
  blocking collectives: 110 us -> 0 us
  waiting for transfers between devices: 78.2 us -> 0 us
  Pallas kernels: 39.8 us -> 99.2 us
  starting transfers between devices: 26.1 us -> 0 us
  between operations: 15.6 us -> 0.64 us
  matrix products: 10.2 us -> 0 us
  other arithmetic: 8.58 us -> 0 us
  local copies, waits for them, and re-layouts: 9.01 us -> 4.72 us
    psum x2 -> x0, blocking collectives: 110 us -> none  [the longest x1 97.1 us: local(): lax.psum((sums[1032:1096] - u_off, jnp.sum(counts[1032:1096, 0:8], axis=1...]
    psum x1 -> x0, waiting for transfers between devices: 68.8 us -> none  [local(): lax.psum((sums[1032:1096] - u_off, jnp.sum(counts[1032:1096, 0:8], axis=1...]
    pallas_call x1, Pallas kernels: 39.8 us -> 99.2 us  [local(): pl.pallas_call(kernel, out_shape=(jax.ShapeDtypeStruct(src.shape, f32), j...]
    all_to_all x3 -> x0, starting transfers between devices: 26.1 us -> none  [the longest x1 11.5 us: local(): lax.all_to_all(request_list.reshape(128, 8), axes, split_axis=0, concat_a...]
    dot_general x5 -> x0, matrix products: 10.2 us -> none  [the longest x1 4.62 us: local(): rsum = jnp.dot(dense, got, precision=hi)]
    all_to_all x3 -> x0, waiting for transfers between devices: 9.35 us -> none  [the longest x1 9.34 us: local(): lax.all_to_all(counts[:1024].reshape(128, 8, LANES), axes, split_axis=0,...]
    reshape x2 -> x0, local copies, waits for them, and re-layouts: 6.74 us -> none  [the longest x1 4.79 us: local(): sums[:1024].reshape(128, 8, 1024)]
    add x7 -> x0, other arithmetic: 3.87 us -> none  [the longest x2 1.76 us: local(): offset_new = off + off_sum / (off_cnt + 1.0)[:, None]]
  transfers between devices with their start and end apart: 5 -> 0, of which waited for: 2 -> 0; matrix products, arithmetic and copies ran while one was open for 7% -> 0% of each run, Pallas kernels for 13% -> 0%
where the time goes in v2:
time: 106 us; the launch traced here: 105 us
  Pallas kernels  99.2 us (94%)
  local copies, waits for them, and re-layouts  4.72 us (4%)
    pallas_call x1, Pallas kernels, local(): pl.pallas_call(kernel, out_shape=(jax.ShapeDtypeStruct(src.shape, f32), j...  99.2 us
    unnamed x3, local copies, waits for them, and re-layouts  4.72 us

profile of v2, /device:TPU:1, one launch (start us, length us, event | category | flops | bytes accessed | tf_op | source)
XLA Modules:
  0.0 104.5 jit_solution(6143826859341828263)
XLA Ops:
  0.6 99.2 %update.1 = (f32[8,1024]{1,0:T(8,128)}, f32[64,1024]{1,0:T(8,128)}, f32[64,1024]{1,0:T(8,128)}) custom-call(bf16[2048,2048]{1,0:T(8,128)(2,1)} %tr_hbm.1, s32[16,128]{1,0:T(8,128)} %bitcast.6, s32[16,128]{1,0:T(8,128)} %bitcast.7, s32[16,128]{1,0:T(8,128)} %bitcast.8, s32[8,128]{1,0:T(8,128)} %bitcast.9, f32[8,1024]{1,0:T(8,128)} %s_ref.1, ...), custom_call_target="tpu_custom_call" | custom-call | tf_op jit(solution)/shard_map/update/pallas_call | solution.py:453
  99.8 1.4 %copy.14 = f32[8,1024]{1,0:T(8,128)} copy(f32[8,1024]{1,0:T(8,128)} %get-tuple-element.6) | data formatting | bytes 65536
  101.2 1.7 %copy.15 = f32[64,1024]{1,0:T(8,128)} copy(f32[64,1024]{1,0:T(8,128)} %get-tuple-element.7) | data formatting | bytes 524288
  102.9 1.7 %copy.16 = f32[64,1024]{1,0:T(8,128)} copy(f32[64,1024]{1,0:T(8,128)} %get-tuple-element.8) | data formatting | bytes 524288

commit v3 on v2

--- a/solution.py
+++ b/solution.py
@@ -12,7 +12,7 @@
 ROWS = 1152
 WIDE = 1024 + LANES
 MESH = pl.DeviceIdType.MESH
-KINDS = (0, 1, 2, 0, 1, 2, 0, 1)
+KINDS = ((0, 1, 2, 0, 1, 2, 0, 1), (1, 2, 0, 1, 2, 0, 1, 2))
 SECOND = ("y", "z", "x")
 THIRD = ("z", "x", "y")
 TN = (((0,), (0,)), ((), ()))
@@ -61,9 +61,9 @@
     snew, rnew, onew,
     tr, hot, table, cb, sb, low, extra,
     grid, b1, b1d, b2, b2d, b3, pick,
-    c2, c3, us, e0, e1, v2, e2, uoff,
+    c2, comb, c3, us, e0, e1, v2, e2, uoff, own_list, far_list,
     ex, off, eo, ho, eh, eh2, eh3, fa, inv,
-    tr_sem, s0s, s0r, s1s, s1r, s2s, s2r, s3s, s3r, us_s, us_r, os_s, os_r, xs_s, xs_r,
+    tr_sem, s0s, s0r, s1s, s1r, s2s, s2r, s3s, s3r, us_s, us_r, os_s, os_r, xs_s, xs_r, ls_s, ls_r,
 ):
     f32, bf16 = jnp.float32, jnp.bfloat16
     group, x = lax.axis_index("src"), lax.axis_index("rcv")
@@ -127,24 +127,30 @@
             for k in (1, 2, 3)
         ]
 
-    def c_x2():
+    def c_x2(a):
+        return [rc(b1d.at[8, step(a, k)], c2.at[k], s2s.at[8, k - 1], s2r.at[8, k - 1], at(a, k)) for k in (1, 2, 3)]
+
+    def c_x3(b):
+        return [rc(comb.at[step(b, k)], c3.at[k - 1], s3s.at[8, k - 1], s3r.at[8, k - 1], at(b, k)) for k in (1, 2, 3)]
+
+    def list_0():
+        return [rc(own_list.at[0], own_list.at[1], ls_s.at[9], ls_r.at[9], twin)]
+
+    def list_1():
         return [
-            rc(b1d.at[8, step("y", k)], c2.at[k], s2s.at[8, k - 1], s2r.at[8, k - 1], at("y", k)) for k in (1, 2, 3)
+            rc(own_list, far_list.at[n, k - 1], ls_s.at[3 * n + k - 1], ls_r.at[3 * n + k - 1], at(ax, k))
+            for n, ax in enumerate("xyz")
+            for k in (1, 2, 3)
         ]
 
-    def c_x3():
-        return [
-            rc(c2.at[:, step("z", k)], c3.at[k - 1], s3s.at[8, k - 1], s3r.at[8, k - 1], at("z", k)) for k in (1, 2, 3)
-        ]
-
     def u_core():
-        return [rc(us.at[1], e0, us_s.at[0], us_r.at[0], twin)]
-
-    def u_y():
-        return [rc(us.at[0, :, k], e1.at[k - 1], us_s.at[k], us_r.at[k], at("y", 4 - k)) for k in (1, 2, 3)]
-
-    def u_z():
-        return [rc(v2.at[k], e2.at[k - 1], us_s.at[3 + k], us_r.at[3 + k], at("z", 4 - k)) for k in (1, 2, 3)]
+        return [rc(us.at[:, :, 1], e0, us_s.at[0], us_r.at[0], twin)]
+
+    def u_near(a):
+        return [rc(us.at[:, k, 0], e1.at[k - 1], us_s.at[k], us_r.at[k], at(a, 4 - k)) for k in (1, 2, 3)]
+
+    def u_far(b):
+        return [rc(v2.at[k], e2.at[k - 1], us_s.at[3 + k], us_r.at[3 + k], at(b, 4 - k)) for k in (1, 2, 3)]
 
     def src_x():
         return [rc(ex.at[x], ex.at[x], xs_s.at[k - 1], xs_r.at[k - 1], at("x", k)) for k in (1, 2, 3)]
@@ -199,21 +205,14 @@
     extra[0:8, 1024:WIDE] = jnp.broadcast_to(count_s, (8, LANES))
     extra[8:72, 1024:WIDE] = jnp.broadcast_to(count_o, (64, LANES))
 
-    asked = list_ref[...].astype(f32)
-    for yy in range(4):
-        for zz in range(4):
-            for xx in range(4):
-                p = (yy * 4 + zz) * 8 + xx
-                even = jnp.broadcast_to(asked[:, p : p + 1], (8, LANES))
-                odd = jnp.broadcast_to(asked[:, p + 4 : p + 5], (8, LANES))
-                own, far = jnp.where(c == 0, even, odd), jnp.where(c == 0, odd, even)
-                r = ((yy * 4 + zz) * 4 + xx) * 8
-                grid[8, 0, yy, zz, xx] = jnp.where(lane == 80 + 8, own, cnt[r : r + 8])
-                q = cnt[512 + r : 520 + r]
-                moved = jnp.where((lane >= 80) & (lane < 88), pltpu.roll(q, 80, 1), jnp.where(lane < 8, 0.0, q))
-                grid[8, 2, yy, zz, xx] = jnp.where(lane == 80 + 8, far, moved)
+    grid[8, 0] = cnt[0:512].reshape(4, 4, 4, 8, LANES)
+    far = cnt[512:1024]
+    far = jnp.where((lane >= 80) & (lane < 88), pltpu.roll(far, 80, 1), jnp.where(lane < 8, 0.0, far))
+    grid[8, 2] = far.reshape(4, 4, 4, 8, LANES)
+    own_list[0] = list_ref[...].astype(f32)
 
     pl.semaphore_wait(barrier, len(peers))
+    start(list_0())
     start(x0(8))
     trig_base(cb, sb)
     load.wait()
@@ -224,14 +223,14 @@
         )
         return jnp.concatenate([own.reshape(16, LANES), b1[n, :, :, p, q].reshape(48, LANES)], axis=0)
 
-    def densify(i, n, kind):
+    def densify(i, n, kind, swap=False):
         def one(m, _):
             p, q = m // 4, lax.rem(m, 4)
             upper, lower = split(rows64(i, n, kind, p, q))
             both = jnp.concatenate([upper, lower], axis=1)
             out = jnp.dot(pick[kind, m], both, preferred_element_type=f32)
             total = out[:, 0:LANES] + out[:, LANES:]
-            if kind == 2:
+            if kind == 2 or swap:
                 b1d[i, q, p] = total
             else:
                 b1d[i, p, q] = total
@@ -240,50 +239,65 @@
         lax.fori_loop(0, 16, one, 0, unroll=4)
 
     def counts_1():
+        wait(list_0())
+        start(list_1())
         wait(x0(8))
+        start(x1(8, 0, 8))
+
+    def lists():
+        wait(list_1())
+        row = lax.broadcasted_iota(jnp.int32, (1024, LANES), 0)
+        col = lax.broadcasted_iota(jnp.int32, (1024, LANES), 1)
+        p, q = row >> 8, (row >> 6) & 3
+        want = (lax.broadcasted_iota(jnp.int32, (1024, 64), 0) & 63).astype(f32)
         for kind in range(3):
-            start(x1(8, kind, 8 + kind))
+            py, pz, px = ((p, q, x), (y, p, q), (p, z, q))[kind]
+            owner = ((py * 4 + pz) * 2 + c) * 4 + px
+            which = jnp.where(col == owner, 1.0, 0.0).astype(bf16)
+            rows = jnp.concatenate([own_list[...].reshape(16, LANES), far_list[kind].reshape(48, LANES)], axis=0)
+            named = lax.dot_general(which, rows.astype(bf16), NT, preferred_element_type=f32)
+            pick[kind] = jnp.where(named == want, 1.0, 0.0).astype(bf16).reshape(16, 64, 64)
+
+    def by_core(f):
+        for core, axes in enumerate((("y", "z"), ("z", "y"))):
+            @pl.when(c == core)
+            def _(axes=axes):
+                f(*axes)
 
     def counts_2():
-        eye = jnp.where(
-            lax.broadcasted_iota(jnp.int32, (64, 64), 0) == lax.broadcasted_iota(jnp.int32, (64, 64), 1), 1.0, 0.0
-        ).astype(bf16)
-        col = lax.broadcasted_iota(jnp.int32, (64, 64), 1).astype(f32)
-        for kind in range(3):
-            wait(x1(8, kind, 8 + kind))
-
-            def one(m, _, kind=kind):
-                rows = rows64(8, 8 + kind, kind, m // 4, lax.rem(m, 4))
-                flipped = jnp.where(rows[:, 88:89] == col, 1.0, 0.0).astype(bf16)
-                pick[kind, m] = lax.dot_general(eye, flipped, NT, preferred_element_type=f32).astype(bf16)
-                return 0
-
-            lax.fori_loop(0, 16, one, 0, unroll=4)
-        densify(8, 8, 0)
-        start(c_x2())
+        wait(x1(8, 0, 8))
+
+        def go(a, b):
+            densify(8, 8, 0, swap=a == "z")
+            start(c_x2(a))
+
+        by_core(go)
 
     def counts_3():
-        wait(c_x2())
-        c2[0] = b1d[8, y]
-        start(c_x3())
+        def go(a, b):
+            wait(c_x2(a))
+            c2[0] = b1d[8, me[a]]
+            total = jnp.zeros((256, LANES), f32)
+            for k in range(4):
+                mm = c2[k].reshape(256, LANES)
+                total = total + pltpu.roll(jnp.where((lane >= 8) & (lane < 72), mm, 0.0), 120, 1)
+                total = total + pltpu.roll(jnp.where(lane < 8, mm, 0.0), 64 + 16 * k, 1)
+                moved = (16 * k + 120) % 128
+                one = jnp.where((lane >= 80) & (lane < 88), mm, 0.0)
+                total = total + (pltpu.roll(one, moved, 1) if moved else one)
+            comb[...] = total.reshape(4, 64, LANES)
+            start(c_x3(b))
+
+        by_core(go)
 
     def counts_4():
-        wait(c_x3())
-        total = jnp.zeros((64, LANES), f32)
-        w0, w1 = total, total
-        for kz in range(4):
-            for ky in range(4):
-                mm = c2[ky, z] if kz == 0 else c3[kz - 1, ky]
-                n = 8 * (kz * 4 + ky)
-                total = total + mm
-                a = jnp.where(lane < 8, mm, 0.0)
-                b = jnp.where((lane >= 80) & (lane < 88), mm, 0.0)
-                w0 = w0 + (pltpu.roll(a, n, 1) if n else a)
-                w1 = w1 + pltpu.roll(b, (n + 48) % 128, 1)
-        offs = jnp.where((lane >= 8) & (lane < 72), total, 0.0)
+        by_core(lambda a, b: wait(c_x3(b)))
+        parts = [comb[jnp.where(c == 0, z, y)], c3[0], c3[1], c3[2]]
+        offs = jnp.where(lane < 64, parts[0] + parts[1] + parts[2] + parts[3], 0.0)
         hits = jnp.sum(offs, axis=1, keepdims=True)
         inv[...] = jnp.broadcast_to(1.0 / (hits + 1.0), (64, LANES))
-        wide = jnp.concatenate([w0, w1, pltpu.roll(offs, 120, 1)], axis=1)
+        high = [jnp.where(lane >= 64, v, 0.0) for v in parts]
+        wide = jnp.concatenate([pltpu.roll(high[0], 64, 1) + high[1], pltpu.roll(high[2], 64, 1) + high[3], offs], axis=1)
         upper, lower = split(wide)
         left = jnp.concatenate([upper, lower], axis=0)
         for h in range(4):
@@ -291,50 +305,86 @@
             both = jnp.concatenate([r1, r2], axis=1)
             out = lax.dot_general(left, jnp.concatenate([both, both], axis=0), TN, preferred_element_type=f32)
             u = out[:, 0:256] + out[:, 256:]
-            us[:, :, :, :, h * 256 : h * 256 + 256] = u[0:256].reshape(2, 4, 4, 8, 256)
+            us[:, :, :, :, h * 256 : h * 256 + 256] = u[0:256].reshape(4, 4, 2, 8, 256)
             uoff[:, h * 256 : h * 256 + 256] = u[256:320]
         start(u_core())
 
     def counts_5():
         wait(u_core())
-        us[0] = us[0] + e0[...]
-        start(u_y())
+        for p in range(4):
+            for q in range(4):
+                us[p, q, 0] = us[p, q, 0] + e0[q, p]
+        by_core(lambda a, b: start(u_near(a)))
 
     def counts_6():
-        wait(u_y())
-        v2[...] = us[0, :, 0] + e1[0] + e1[1] + e1[2]
-        start(u_z())
+        by_core(lambda a, b: wait(u_near(a)))
+        v2[...] = us[:, 0, 0] + e1[0] + e1[1] + e1[2]
+        by_core(lambda a, b: start(u_far(b)))
 
     def counts_7():
-        wait(u_z())
+        by_core(lambda a, b: wait(u_far(b)))
+        ex[x, :, 0:1024] = extra[0:8, 0:1024] - (v2[0] + e2[0] + e2[1] + e2[2])
+        ex[x, :, 1024:WIDE] = extra[0:8, 1024:WIDE]
+        start(src_x())
+
+    def each_core(i, f):
+        for core in (0, 1):
+            @pl.when(c == core)
+            def _(kind=KINDS[core][i]):
+                f(kind)
 
     def w0(i):
         wait(x0(i))
-        start(x1(i, KINDS[i], i))
+        each_core(i, lambda kind: start(x1(i, kind, i)))
 
     def w1(i):
-        wait(x1(i, KINDS[i], i))
-        densify(i, i, KINDS[i])
-        start(x2(i, KINDS[i]))
+        def go(kind):
+            wait(x1(i, kind, i))
+            densify(i, i, kind)
+            start(x2(i, kind))
+
+        each_core(i, go)
 
     def w2(i):
-        wait(x2(i, KINDS[i]))
-        b2d[i] = b1d[i, me[SECOND[KINDS[i]]]] + b2[i, 0] + b2[i, 1] + b2[i, 2]
-        start(x3(i, KINDS[i]))
+        def go(kind):
+            wait(x2(i, kind))
+            b2d[i] = b1d[i, me[SECOND[kind]]] + b2[i, 0] + b2[i, 1] + b2[i, 2]
+            start(x3(i, kind))
+
+        each_core(i, go)
 
     def w3(i):
-        wait(x3(i, KINDS[i]))
-        total = b2d[i, me[THIRD[KINDS[i]]]] + b3[i, 0] + b3[i, 1] + b3[i, 2]
-        cols = slice(i * LANES, (i + 1) * LANES)
-        rnew[:, cols] = (r_ref[:, cols] + total) * inv[...]
-
-    mid = {0: [counts_1], 1: [lambda: w0(0)], 2: [lambda: w0(1), counts_3], 3: [lambda: w0(2), counts_4],
-           4: [lambda: w0(3), counts_5], 5: [lambda: w0(4), counts_6], 6: [lambda: w0(5), counts_7], 7: [lambda: w0(6)]}
-    end = {1: [counts_2], 3: [lambda: w1(0)], 4: [lambda: w1(1)], 5: [lambda: w1(2), lambda: w2(0)],
-           6: [lambda: w1(3), lambda: w2(1)], 7: [lambda: w1(4), lambda: w2(2), lambda: w3(0)]}
+        def go(kind):
+            wait(x3(i, kind))
+            total = b2d[i, me[THIRD[kind]]] + b3[i, 0] + b3[i, 1] + b3[i, 2]
+            cols = slice(i * LANES, (i + 1) * LANES)
+            rnew[:, cols] = (r_ref[:, cols] + total) * inv[...]
+
+        each_core(i, go)
+
+    def later(f, n):
+        return lambda: f(n)
+
+    first = {2: [counts_2], 4: [counts_3], 5: [counts_4], 6: [counts_5]}
+    mid = {
+        0: [counts_1], 1: [later(w0, 0)], 2: [later(w0, 1)], 3: [later(w0, 2)], 4: [later(w0, 3), later(w2, 0)],
+        5: [later(w0, 4), later(w2, 1)], 6: [later(w0, 5), later(w2, 2)], 7: [later(w0, 6), later(w2, 3), counts_6],
+    }
+    end = {
+        1: [lists], 2: [later(w1, 0)], 3: [later(w1, 1)], 4: [later(w1, 2)], 5: [later(w1, 3)],
+        6: [later(w1, 4), later(w3, 0)], 7: [later(w1, 5), later(w3, 1)],
+    }
+
+    def point(i, table_of):
+        for n, todo in table_of.items():
+            @pl.when(i == n)
+            def _(todo=todo):
+                for f in todo:
+                    f()
 
     def chunk(i, _):
         at_lane = pl.multiple_of(i * LANES, LANES)
+        point(i, first)
         chunk_table(i, range(0, NS, 16), cb, sb, table)
         for r in range(0, NS, 256):
             spec = jnp.dot(tr[r : r + 256, :], table[...], preferred_element_type=f32)
@@ -348,11 +398,7 @@
         for r in (NS, NS + LANES):
             low[r : r + 72, 0:LANES] = upper
             low[r : r + 72, LANES:] = lower
-        for n, todo in mid.items():
-            @pl.when(i == n)
-            def _(todo=todo):
-                for f in todo:
-                    f()
+        point(i, mid)
         for half in (0, 1):
             out = jnp.dot(hot[half * 512 : half * 512 + 512, :], low[...], preferred_element_type=f32)
             grid[i, 2 * half] = (out[:, 0:LANES] + out[:, LANES:]).reshape(4, 4, 4, 8, LANES)
@@ -368,46 +414,47 @@
 
     lax.fori_loop(0, 8, chunk, 0)
 
-    ex[x, :, 0:1024] = extra[0:8, 0:1024] - (v2[0] + e2[0] + e2[1] + e2[2])
-    ex[x, :, 1024:WIDE] = extra[0:8, 1024:WIDE]
-    start(src_x())
     off[:, :, :, 0:1024] = (extra[8:72, 0:1024] - uoff[...]).reshape(2, 4, 8, 1024)
     off[:, :, :, 1024:WIDE] = extra[8:72, 1024:WIDE].reshape(2, 4, 8, LANES)
     start(off_core())
+    w2(4)
+    w3(2)
     w0(7)
     wait(off_core())
     ho[...] = off[c] + eo[...]
     start(off_x())
-    w1(5)
-    w2(3)
-    w3(1)
+    w3(3)
+    w1(6)
+    counts_7()
     wait(off_x())
     eh2[y] = ho[x] + eh[0] + eh[1] + eh[2]
     start(off_y())
-    w1(6)
-    w2(4)
-    w3(2)
+    w2(5)
     wait(off_y())
     eh3[z] = eh2[0] + eh2[1] + eh2[2] + eh2[3]
     start(off_z())
     w1(7)
-    w2(5)
-    w3(3)
+    w3(4)
     wait(off_z())
     fa[c, x] = eh3[0] + eh3[1] + eh3[2] + eh3[3]
     start(off_all())
     w2(6)
-    w3(4)
-    w2(7)
     w3(5)
     wait(src_x())
     total = ex[0] + ex[1] + ex[2] + ex[3]
     snew[...] = s_ref[...] + total[:, 0:1024] / (total[:, 1024:1025] + 1.0)
+    w2(7)
+    w3(6)
     wait(off_all())
     total = fa[...].reshape(64, WIDE)
     onew[...] = o_ref[...] + total[:, 0:1024] / (total[:, 1024:1025] + 1.0)
-    w3(6)
     w3(7)
+
+
+def hand_over(a, b, d, oa, ob, od):
+    oa[...] = a[...]
+    ob[...] = b[...]
+    od[...] = d[...]
 
 
 def local(traces, trace_source, trace_offset, trace_slot, request_list, src, rcv, off):
@@ -423,20 +470,23 @@
         pltpu.VMEM((NS + 256, 256), bf16),
         pltpu.VMEM((72, WIDE), f32),
         pltpu.VMEM((9, 3, 4, 4, 4, 8, LANES), f32),
-        pltpu.VMEM((11, 3, 2, 4, 4, 8, LANES), f32),
+        pltpu.VMEM((9, 3, 2, 4, 4, 8, LANES), f32),
         pltpu.VMEM((9, 4, 4, 64, LANES), f32),
         pltpu.VMEM((8, 3, 4, 64, LANES), f32),
         pltpu.VMEM((8, 4, 64, LANES), f32),
         pltpu.VMEM((8, 3, 64, LANES), f32),
         pltpu.VMEM((3, 16, 64, 64), bf16),
         pltpu.VMEM((4, 4, 64, LANES), f32),
-        pltpu.VMEM((3, 4, 64, LANES), f32),
-        pltpu.VMEM((2, 4, 4, 8, 1024), f32),
+        pltpu.VMEM((4, 64, LANES), f32),
+        pltpu.VMEM((3, 64, LANES), f32),
+        pltpu.VMEM((4, 4, 2, 8, 1024), f32),
         pltpu.VMEM((4, 4, 8, 1024), f32),
         pltpu.VMEM((3, 4, 8, 1024), f32),
         pltpu.VMEM((4, 8, 1024), f32),
         pltpu.VMEM((3, 8, 1024), f32),
         pltpu.VMEM((64, 1024), f32),
+        pltpu.VMEM((2, 8, LANES), f32),
+        pltpu.VMEM((3, 3, 2, 8, LANES), f32),
         pltpu.VMEM((4, 8, WIDE), f32),
         pltpu.VMEM((2, 4, 8, WIDE), f32),
         pltpu.VMEM((4, 8, WIDE), f32),
@@ -447,16 +497,13 @@
         pltpu.VMEM((2, 4, 8, WIDE), f32),
         pltpu.VMEM((64, LANES), f32),
         dma,
-        dma((9,)), dma((9,)), dma((11, 3)), dma((11, 3)), dma((9, 3)), dma((9, 3)), dma((9, 3)), dma((9, 3)),
-        dma((7,)), dma((7,)), dma((17,)), dma((17,)), dma((3,)), dma((3,)),
+        dma((9,)), dma((9,)), dma((9, 3)), dma((9, 3)), dma((9, 3)), dma((9, 3)), dma((9, 3)), dma((9, 3)),
+        dma((7,)), dma((7,)), dma((17,)), dma((17,)), dma((3,)), dma((3,)), dma((10,)), dma((10,)),
     ]
-    return pl.pallas_call(
+    shapes = tuple(jax.ShapeDtypeStruct(v.shape, f32) for v in (src, rcv, off))
+    parts = pl.pallas_call(
         kernel,
-        out_shape=(
-            jax.ShapeDtypeStruct(src.shape, f32),
-            jax.ShapeDtypeStruct(rcv.shape, f32),
-            jax.ShapeDtypeStruct(off.shape, f32),
-        ),
+        out_shape=shapes,
         in_specs=[pl.BlockSpec(memory_space=pl.ANY)] + [vmem] * 7,
         out_specs=(vmem, vmem, vmem),
         scratch_shapes=scratch,
@@ -472,6 +519,13 @@
         rcv,
         off,
     )
+    return pl.pallas_call(
+        hand_over,
+        out_shape=shapes,
+        in_specs=[vmem] * 3,
+        out_specs=(vmem,) * 3,
+        name="hand_over",
+    )(*parts)
 
 
 def solution(mesh):

time: 106 us -> 87.3 us (0.82)
  Pallas kernels: 99.2 us -> 85.4 us
  local copies, waits for them, and re-layouts: 4.72 us -> 0 us
    pallas_call x1 -> x2, Pallas kernels: 99.2 us -> 85.4 us  [the longest x1 83.5 us: local(): pl.pallas_call(kernel, out_shape=shapes, in_specs=[pl.BlockSpec(memory_sp...]
    unnamed x3 -> x0, local copies, waits for them, and re-layouts: 4.72 us -> none
where the time goes in v3:
time: 87.3 us; the launch traced here: 86 us
  Pallas kernels  85.4 us (98%)
    pallas_call x1, Pallas kernels, local(): pl.pallas_call(kernel, out_shape=shapes, in_specs=[pl.BlockSpec(memory_sp...  83.5 us
    pallas_call x1, Pallas kernels, local(): pl.pallas_call(hand_over, out_shape=shapes, in_specs=[vmem] * 3, out_spec...  1.87 us

profile of v3, /device:TPU:1, one launch (start us, length us, event | category | flops | bytes accessed | tf_op | source)
XLA Modules:
  0.0 86.0 jit_solution(8473497785442165837)
XLA Ops:
  0.6 83.5 %update.1 = (f32[8,1024]{1,0:T(8,128)}, f32[64,1024]{1,0:T(8,128)}, f32[64,1024]{1,0:T(8,128)}) custom-call(bf16[2048,2048]{1,0:T(8,128)(2,1)} %tr_hbm.1, s32[16,128]{1,0:T(8,128)} %bitcast.6, s32[16,128]{1,0:T(8,128)} %bitcast.7, s32[16,128]{1,0:T(8,128)} %bitcast.8, s32[8,128]{1,0:T(8,128)} %bitcast.9, f32[8,1024]{1,0:T(8,128)} %s_ref.1, ...), custom_call_target="tpu_custom_call" | custom-call | tf_op jit(solution)/shard_map/update/pallas_call | solution.py:504
  84.1 1.9 %hand_over.1 = (f32[8,1024]{1,0:T(8,128)}, f32[64,1024]{1,0:T(8,128)}, f32[64,1024]{1,0:T(8,128)}) custom-call(f32[8,1024]{1,0:T(8,128)} %get-tuple-element.6.a, f32[64,1024]{1,0:T(8,128)} %get-tuple-element.7.b, f32[64,1024]{1,0:T(8,128)} %get-tuple-element.8.d), custom_call_target="tpu_custom_call" | custom-call | tf_op jit(solution)/shard_map/hand_over/pallas_call | solution.py:522

commit v4 on v3

--- a/solution.py
+++ b/solution.py
@@ -365,14 +365,29 @@
     def later(f, n):
         return lambda: f(n)
 
-    first = {2: [counts_2], 4: [counts_3], 5: [counts_4], 6: [counts_5]}
+    first = {
+        2: [lists],
+        3: [later(w1, 0)],
+        4: [later(w1, 1)],
+        5: [later(w1, 2), later(w2, 0)],
+        6: [later(w1, 3), later(w2, 1)],
+        7: [later(w1, 4), later(w2, 2)],
+    }
     mid = {
-        0: [counts_1], 1: [later(w0, 0)], 2: [later(w0, 1)], 3: [later(w0, 2)], 4: [later(w0, 3), later(w2, 0)],
-        5: [later(w0, 4), later(w2, 1)], 6: [later(w0, 5), later(w2, 2)], 7: [later(w0, 6), later(w2, 3), counts_6],
+        0: [counts_1],
+        1: [later(w0, 0)],
+        2: [later(w0, 1)],
+        3: [later(w0, 2)],
+        4: [later(w0, 3)],
+        5: [later(w0, 4)],
+        6: [later(w0, 5), later(w3, 0)],
+        7: [later(w0, 6), later(w3, 1)],
     }
     end = {
-        1: [lists], 2: [later(w1, 0)], 3: [later(w1, 1)], 4: [later(w1, 2)], 5: [later(w1, 3)],
-        6: [later(w1, 4), later(w3, 0)], 7: [later(w1, 5), later(w3, 1)],
+        2: [counts_2],
+        4: [counts_3],
+        5: [counts_4],
+        6: [counts_5],
     }
 
     def point(i, table_of):
@@ -417,37 +432,40 @@
     off[:, :, :, 0:1024] = (extra[8:72, 0:1024] - uoff[...]).reshape(2, 4, 8, 1024)
     off[:, :, :, 1024:WIDE] = extra[8:72, 1024:WIDE].reshape(2, 4, 8, LANES)
     start(off_core())
-    w2(4)
+    w1(5)
+    w2(3)
+    counts_6()
+    w0(7)
     w3(2)
-    w0(7)
     wait(off_core())
     ho[...] = off[c] + eo[...]
     start(off_x())
+    w1(6)
+    w2(4)
     w3(3)
-    w1(6)
     counts_7()
     wait(off_x())
     eh2[y] = ho[x] + eh[0] + eh[1] + eh[2]
     start(off_y())
+    w1(7)
     w2(5)
+    w3(4)
     wait(off_y())
     eh3[z] = eh2[0] + eh2[1] + eh2[2] + eh2[3]
     start(off_z())
-    w1(7)
-    w3(4)
+    w2(6)
+    w3(5)
     wait(off_z())
     fa[c, x] = eh3[0] + eh3[1] + eh3[2] + eh3[3]
     start(off_all())
-    w2(6)
-    w3(5)
-    wait(src_x())
-    total = ex[0] + ex[1] + ex[2] + ex[3]
-    snew[...] = s_ref[...] + total[:, 0:1024] / (total[:, 1024:1025] + 1.0)
     w2(7)
     w3(6)
     wait(off_all())
     total = fa[...].reshape(64, WIDE)
     onew[...] = o_ref[...] + total[:, 0:1024] / (total[:, 1024:1025] + 1.0)
+    wait(src_x())
+    total = ex[0] + ex[1] + ex[2] + ex[3]
+    snew[...] = s_ref[...] + total[:, 0:1024] / (total[:, 1024:1025] + 1.0)
     w3(7)
 
 

time: 87.3 us -> 84.1 us (0.963); the launches traced: 86 us -> 83.9 us
  Pallas kernels: 85.4 us -> 83.3 us
    pallas_call x1, Pallas kernels: 83.5 us -> 81.4 us  [local(): pl.pallas_call(kernel, out_shape=shapes, in_specs=[pl.BlockSpec(memory_sp...]
where the time goes in v4:
time: 84.1 us; the launch traced here: 83.9 us
  Pallas kernels  83.3 us (99%)
    pallas_call x1, Pallas kernels, local(): pl.pallas_call(kernel, out_shape=shapes, in_specs=[pl.BlockSpec(memory_sp...  81.4 us
    pallas_call x1, Pallas kernels, local(): pl.pallas_call(hand_over, out_shape=shapes, in_specs=[vmem] * 3, out_spec...  1.87 us

profile of v4, /device:TPU:1, one launch (start us, length us, event | category | flops | bytes accessed | tf_op | source)
XLA Modules:
  0.0 83.9 jit_solution(14429087612180342670)
XLA Ops:
  0.6 81.4 %update.1 = (f32[8,1024]{1,0:T(8,128)}, f32[64,1024]{1,0:T(8,128)}, f32[64,1024]{1,0:T(8,128)}) custom-call(bf16[2048,2048]{1,0:T(8,128)(2,1)} %tr_hbm.1, s32[16,128]{1,0:T(8,128)} %bitcast.6, s32[16,128]{1,0:T(8,128)} %bitcast.7, s32[16,128]{1,0:T(8,128)} %bitcast.8, s32[8,128]{1,0:T(8,128)} %bitcast.9, f32[8,1024]{1,0:T(8,128)} %s_ref.1, ...), custom_call_target="tpu_custom_call" | custom-call | tf_op jit(solution)/shard_map/update/pallas_call | solution.py:522
  82.0 1.9 %hand_over.1 = (f32[8,1024]{1,0:T(8,128)}, f32[64,1024]{1,0:T(8,128)}, f32[64,1024]{1,0:T(8,128)}) custom-call(f32[8,1024]{1,0:T(8,128)} %get-tuple-element.6.a, f32[64,1024]{1,0:T(8,128)} %get-tuple-element.7.b, f32[64,1024]{1,0:T(8,128)} %get-tuple-element.8.d), custom_call_target="tpu_custom_call" | custom-call | tf_op jit(solution)/shard_map/hand_over/pallas_call | solution.py:540

commit v5 on v4

--- a/solution.py
+++ b/solution.py
@@ -367,27 +367,23 @@
 
     first = {
         2: [lists],
+    }
+    mid = {
+        0: [counts_1],
         3: [later(w1, 0)],
         4: [later(w1, 1)],
         5: [later(w1, 2), later(w2, 0)],
         6: [later(w1, 3), later(w2, 1)],
         7: [later(w1, 4), later(w2, 2)],
     }
-    mid = {
-        0: [counts_1],
+    end = {
         1: [later(w0, 0)],
-        2: [later(w0, 1)],
+        2: [later(w0, 1), counts_2],
         3: [later(w0, 2)],
-        4: [later(w0, 3)],
-        5: [later(w0, 4)],
-        6: [later(w0, 5), later(w3, 0)],
+        4: [later(w0, 3), counts_3],
+        5: [later(w0, 4), counts_4],
+        6: [later(w0, 5), later(w3, 0), counts_5],
         7: [later(w0, 6), later(w3, 1)],
-    }
-    end = {
-        2: [counts_2],
-        4: [counts_3],
-        5: [counts_4],
-        6: [counts_5],
     }
 
     def point(i, table_of):
@@ -432,9 +428,9 @@
     off[:, :, :, 0:1024] = (extra[8:72, 0:1024] - uoff[...]).reshape(2, 4, 8, 1024)
     off[:, :, :, 1024:WIDE] = extra[8:72, 1024:WIDE].reshape(2, 4, 8, LANES)
     start(off_core())
+    counts_6()
     w1(5)
     w2(3)
-    counts_6()
     w0(7)
     w3(2)
     wait(off_core())
@@ -442,27 +438,27 @@
     start(off_x())
     w1(6)
     w2(4)
-    w3(3)
     counts_7()
     wait(off_x())
     eh2[y] = ho[x] + eh[0] + eh[1] + eh[2]
     start(off_y())
+    w3(3)
     w1(7)
     w2(5)
-    w3(4)
     wait(off_y())
     eh3[z] = eh2[0] + eh2[1] + eh2[2] + eh2[3]
     start(off_z())
+    w3(4)
     w2(6)
-    w3(5)
     wait(off_z())
     fa[c, x] = eh3[0] + eh3[1] + eh3[2] + eh3[3]
     start(off_all())
+    w3(5)
     w2(7)
-    w3(6)
     wait(off_all())
     total = fa[...].reshape(64, WIDE)
     onew[...] = o_ref[...] + total[:, 0:1024] / (total[:, 1024:1025] + 1.0)
+    w3(6)
     wait(src_x())
     total = ex[0] + ex[1] + ex[2] + ex[3]
     snew[...] = s_ref[...] + total[:, 0:1024] / (total[:, 1024:1025] + 1.0)

time: 84.1 us -> 84.9 us (level)
    pallas_call x1, Pallas kernels: 81.4 us -> 82.3 us  [local(): pl.pallas_call(kernel, out_shape=shapes, in_specs=[pl.BlockSpec(memory_sp...]
where the time goes in v5:
time: 84.9 us; the launch traced here: 84.8 us
  Pallas kernels  84.1 us (99%)
    pallas_call x1, Pallas kernels, local(): pl.pallas_call(kernel, out_shape=shapes, in_specs=[pl.BlockSpec(memory_sp...  82.3 us
    pallas_call x1, Pallas kernels, local(): pl.pallas_call(hand_over, out_shape=shapes, in_specs=[vmem] * 3, out_spec...  1.87 us

profile of v5, /device:TPU:1, one launch (start us, length us, event | category | flops | bytes accessed | tf_op | source)
XLA Modules:
  0.0 84.8 jit_solution(3374626109719525691)
XLA Ops:
  0.6 82.3 %update.1 = (f32[8,1024]{1,0:T(8,128)}, f32[64,1024]{1,0:T(8,128)}, f32[64,1024]{1,0:T(8,128)}) custom-call(bf16[2048,2048]{1,0:T(8,128)(2,1)} %tr_hbm.1, s32[16,128]{1,0:T(8,128)} %bitcast.6, s32[16,128]{1,0:T(8,128)} %bitcast.7, s32[16,128]{1,0:T(8,128)} %bitcast.8, s32[8,128]{1,0:T(8,128)} %bitcast.9, f32[8,1024]{1,0:T(8,128)} %s_ref.1, ...), custom_call_target="tpu_custom_call" | custom-call | tf_op jit(solution)/shard_map/update/pallas_call | solution.py:518
  82.9 1.9 %hand_over.1 = (f32[8,1024]{1,0:T(8,128)}, f32[64,1024]{1,0:T(8,128)}, f32[64,1024]{1,0:T(8,128)}) custom-call(f32[8,1024]{1,0:T(8,128)} %get-tuple-element.6.a, f32[64,1024]{1,0:T(8,128)} %get-tuple-element.7.b, f32[64,1024]{1,0:T(8,128)} %get-tuple-element.8.d), custom_call_target="tpu_custom_call" | custom-call | tf_op jit(solution)/shard_map/hand_over/pallas_call | solution.py:536
